TPU v7x, 32 devices: a whole 2x2x4 slice. The times are simulated.
32 devices in a mesh: groups: 1, seq: 32 (over z, y, x, core).
Axes of the slice: x: 2, y: 2, z: 4, core: 2. Of those that a mesh axis runs over, the one named last changes fastest.
Arguments:
- tokens: bfloat16 [4096, 1536], P(('groups', 'seq')), may hold values from -6 to 6
- state_rates: float32 [2, 64], replicated, may hold values from -40 to 40, as said below
- coupling: float32 [2, 64], replicated, may hold values from -6 to 6
- in_proj: float32 [2, 64, 1536], replicated, may hold values from -120 to 120
- out_proj: float32 [2, 64, 1536], replicated, may hold values from -0.01171875 to 0.01171875
- skip_gain: float32 [1536], replicated, may hold values from -4 to 4
- mix_weight: bfloat16 [1536, 3072], P('seq'), may hold values from -0.15625 to 0.15625
Outputs:
- glu_output: bfloat16 [4096, 1536], P(('groups', 'seq'))
Inputs may be any that keep to these rules, and one draw needn't show every extreme that they name: state_rates[0] is negative, between -12 and -1 / 4096; state_rates[1] lies within -40 to 40.
All inputs are finite; a program needn't handle non-finite values.
Results may differ from a plain program's by a relative error of at most 0.0051.
Values may be sent and summed in bfloat16 or wider, within the bound.
No kernel may reach another device: no remote copies, remote signals or barrier semaphores. Data moves between devices by JAX's collectives and lax.ppermute only.
A program may use at most 64 MiB of HBM per device.

v0:
```python
import math

import jax
import jax.numpy as jnp
from jax import lax
from jax.sharding import PartitionSpec as P

PRECISE = lax.Precision.HIGHEST


def phase_of(numerator, period):
    wrapped = numerator % period
    wrapped = jnp.where(wrapped > period // 2, wrapped - period, wrapped)
    return wrapped.astype(jnp.float32) * (-2.0 * math.pi / period)


def complex_mul(first, second):
    return (
        first[0] * second[0] - first[1] * second[1],
        first[0] * second[1] + first[1] * second[0],
    )


def complex_div(first, second):
    norm_sq = second[0] * second[0] + second[1] * second[1]
    return (
        (first[0] * second[0] + first[1] * second[1]) / norm_sq,
        (first[1] * second[0] - first[0] * second[1]) / norm_sq,
    )


def real_form(pair_real, pair_imag):
    upper = jnp.concatenate([pair_real, pair_imag], axis=1)
    lower = jnp.concatenate([-pair_imag, pair_real], axis=1)
    return jnp.concatenate([upper, lower], axis=0)


def cauchy_right(coupling, in_proj, out_proj):
    in_pair = (in_proj[0], in_proj[1])
    out_pair = (out_proj[0], out_proj[1])
    low_pair = (coupling[0][:, None], coupling[1][:, None])
    low_conj = (low_pair[0], -low_pair[1])
    pair_cb = complex_mul(out_pair, in_pair)
    pair_cp = complex_mul(out_pair, low_pair)
    pair_pb = complex_mul(low_conj, in_pair)
    pair_pp = low_pair[0] * low_pair[0] + low_pair[1] * low_pair[1]
    return [
        real_form(pair_cb[0], pair_cb[1]),
        real_form(pair_cp[0], pair_cp[1]),
        real_form(pair_pb[0], pair_pb[1]),
        real_form(pair_pp, jnp.zeros_like(pair_pp)),
    ]


def response(frequency, full_len, state_rates, right_list):
    half_turn = 0.5 * phase_of(frequency, full_len)
    cos_half = jnp.cos(half_turn)[:, None]
    sin_half = jnp.sin(half_turn)[:, None]
    decay_rate = -state_rates[0][None, :]
    spin_rate = state_rates[1][None, :]
    real_part = cos_half * decay_rate
    imag_part = -(2.0 * sin_half + cos_half * spin_rate)
    inv_norm = 1.0 / (real_part * real_part + imag_part * imag_part)
    cauchy_left = jnp.concatenate([real_part * inv_norm, -imag_part * inv_norm], axis=1)
    term_list = []
    for matrix in right_list:
        summed = jnp.dot(cauchy_left, matrix, precision=PRECISE)
        half_cols = matrix.shape[1] // 2
        term_list.append((summed[:, :half_cols], summed[:, half_cols:]))
    term_cb, term_cp, term_pb, term_pp = term_list
    numerator = complex_mul(term_cp, term_pb)
    denominator = (1.0 + cos_half * term_pp[0], cos_half * term_pp[1])
    fraction = complex_div(numerator, denominator)
    bracket = (term_cb[0] - cos_half * fraction[0], term_cb[1] - cos_half * fraction[1])
    return complex_mul((cos_half, -sin_half), bracket)


def dft_table_of(length, direction):
    position = jnp.arange(length, dtype=jnp.int32)
    phases = phase_of(direction * position[:, None] * position[None, :], length)
    cos_table = jnp.cos(phases)
    sin_table = jnp.sin(phases)
    return jnp.stack(
        [jnp.stack([cos_table, -sin_table], 1), jnp.stack([sin_table, cos_table], 1)], 0
    )


def transform(signal, length, direction):
    return jnp.einsum("ascb,ckbh->aksh", dft_table_of(length, direction), signal, precision=PRECISE)


def block_tables(seq_count):
    block_index = jnp.arange(seq_count, dtype=jnp.int32)
    pair_index = jnp.arange(2 * seq_count, dtype=jnp.int32)
    forward_phase = phase_of(pair_index[:, None] * block_index[None, :], 2 * seq_count)
    forward_table = jnp.concatenate([jnp.cos(forward_phase), jnp.sin(forward_phase)], 0)
    inverse_phase = phase_of(-(block_index[:, None] * pair_index[None, :]), 2 * seq_count)
    inverse_table = jnp.concatenate([jnp.cos(inverse_phase), -jnp.sin(inverse_phase)], 1)
    return (forward_table, inverse_table)


def twiddled(signal, first_index, second_index, full_len, direction):
    phases = phase_of(direction * first_index[:, None] * second_index[None, :], full_len)[
        :, :, None
    ]
    turned = complex_mul((signal[0], signal[1]), (jnp.cos(phases), jnp.sin(phases)))
    return jnp.stack(turned)


def shards(tokens, state_rates, coupling, in_proj, out_proj, skip_gain, mix_weight):
    seq_count = lax.axis_size("seq")
    seq_place = lax.axis_index("seq")
    tok_rows, channels = tokens.shape
    full_len = 2 * tok_rows * seq_count
    forward_table, inverse_table = block_tables(seq_count)
    pair_index = jnp.arange(2 * seq_count, dtype=jnp.int32)
    all_times = jnp.arange(tok_rows, dtype=jnp.int32)
    per_device = tok_rows // seq_count
    columns = lax.all_to_all(tokens[None], "seq", split_axis=1, concat_axis=0, tiled=True)
    spread = jnp.dot(
        forward_table,
        columns.astype(jnp.float32).reshape(seq_count, per_device * channels),
        precision=PRECISE,
    )
    spread = spread.reshape(2, 2 * seq_count, per_device, channels)
    local_time = seq_place * per_device + jnp.arange(per_device, dtype=jnp.int32)
    spread = twiddled(spread, pair_index, local_time, full_len, 1)
    gathered = lax.all_to_all(spread, "seq", split_axis=1, concat_axis=2, tiled=True)
    spectrum = transform(gathered, tok_rows, 1)
    pair_here = 2 * seq_place + jnp.arange(2, dtype=jnp.int32)
    frequency = (pair_here[:, None] + 2 * seq_count * all_times[None, :]).reshape(-1)
    right_list = cauchy_right(coupling, in_proj, out_proj)
    kernel_real, kernel_imag = response(frequency, full_len, state_rates, right_list)
    kernel_pair = (
        kernel_real.reshape(2, tok_rows, channels),
        kernel_imag.reshape(2, tok_rows, channels),
    )
    product = jnp.stack(complex_mul(kernel_pair, (spectrum[0], spectrum[1])))
    inverse = transform(product, tok_rows, -1)
    inverse = twiddled(inverse, pair_here, all_times, full_len, -1)
    returned = lax.all_to_all(inverse, "seq", split_axis=2, concat_axis=1, tiled=True)
    conv_out = jnp.dot(
        inverse_table, returned.reshape(4 * seq_count, per_device * channels), precision=PRECISE
    )
    conv_out = conv_out.reshape(seq_count, per_device, channels) * (1.0 / full_len)
    pre_act = conv_out + skip_gain * columns.astype(jnp.float32)
    activation = jax.nn.gelu(pre_act, approximate=False).astype(jnp.bfloat16)
    act_rows = lax.all_to_all(activation, "seq", split_axis=0, concat_axis=1, tiled=True)[0]
    projected = jnp.dot(
        act_rows,
        lax.all_gather(mix_weight, "seq", axis=0, tiled=True),
        preferred_element_type=jnp.float32,
    )
    return (projected[:, :channels] * jax.nn.sigmoid(projected[:, channels:])).astype(jnp.bfloat16)


def solution(mesh):
    placed = (P(("groups", "seq"), None), P(), P(), P(), P(), P(), P("seq", None))
    return jax.shard_map(
        shards, mesh=mesh, in_specs=placed, out_specs=P(("groups", "seq"), None), check_vma=False
    )
```

profile of v0, /device:TPU:0, one launch (start us, length us, event | category | flops | bytes accessed | tf_op | source)
XLA Modules:
  0.0 290.8 jit_solution(13883926220681180937)
XLA Ops:
  6.5 1.6 copy.107
  8.1 0.5 broadcast.842
  8.7 3.0 %reduce.4 = bf16[128,1536]{1,0:T(8,128)(2,1)S(1)} reduce(bf16[128,1,1536]{2,1,0:T(2,128)(2,1)S(1)} %bitcast.155, bf16[]{:T(256)} %broadcast.842), dimensions={1}, to_apply=%bitcast.146.reduce_sub_computation | reduce | bytes 786434
  11.7 1.0 reshape.574
  12.7 7.3 %all-to-all-start = ((bf16[32,2,3072]{2,1,0:T(2,128)(2,1)}), bf16[32,2,3072]{2,1,0:T(2,128)(2,1)S(1)}, u32[]{:S(2)}, u32[]{:S(2)}) async-start(bf16[32,2,3072]{2,1,0:T(2,128)(2,1)} %reshape.574), calls=%async_computation | async-start | bytes 786432 | tf_op jit(solution)/shard_map/all_to_all | solution.py:119
  20.3 0.5 all-gather.2.cloned.1.call-update
  21.2 12.1 %all-to-all-done = bf16[32,2,3072]{2,1,0:T(2,128)(2,1)S(1)} async-done(((bf16[32,2,3072]{2,1,0:T(2,128)(2,1)}), bf16[32,2,3072]{2,1,0:T(2,128)(2,1)S(1)}, u32[]{:S(2)}, u32[]{:S(2)}) %all-to-all-start) | async-done | bytes 393248 | tf_op jit(solution)/shard_map/all_to_all | solution.py:119
  33.2 0.3 reshape.575
  33.6 2.2 bitcast_reduce_fusion
  36.1 1.5 fusion.85
  37.6 1.4 fusion.142
  39.0 1.1 squeeze.29
  40.1 2.4 squeeze.30
  42.5 0.8 fusion.28
  43.3 2.5 pad_maximum_fusion
  45.7 3.2 %all-to-all-start.1 = ((f32[2,64,4,1536]{3,2,0,1:T(4,128)}), f32[2,64,4,1536]{3,2,0,1:T(4,128)S(1)}, u32[]{:S(2)}, u32[]{:S(2)}) async-start(f32[2,64,4,1536]{3,2,0,1:T(4,128)} %pad_maximum_fusion), calls=%async_computation.1 | async-start | bytes 6291456 | tf_op jit(solution)/shard_map/all_to_all | solution.py:128
  49.5 1.7 fusion.140
  51.2 2.7 fusion.12
  53.9 2.7 fusion.20
  56.6 2.7 fusion.4
  59.5 0.6 multiply_add_fusion.3
  60.1 2.1 multiply_subtract_fusion.2
  62.2 1.4 multiply_add_fusion.2
  63.6 3.0 %copy.80 = f32[1,2,128,1536]{2,3,0,1:T(8,128)} copy(f32[1,2,128,1536]{3,2,1,0:T(8,128)} %bitcast.152) | data formatting | bytes 3145728 | tf_op jit(solution)/shard_map/reshape | solution.py:136
  66.6 3.0 %copy.79 = f32[1,2,128,1536]{2,3,0,1:T(8,128)} copy(f32[1,2,128,1536]{3,2,1,0:T(8,128)} %bitcast.153) | data formatting | bytes 3145728 | tf_op jit(solution)/shard_map/reshape | solution.py:135
  69.9 0.3 fusion.71
  70.2 0.3 fusion.76
  70.6 0.7 maximum_bitcast_fusion.8
  71.4 86.3 %all-to-all-done.1 = f32[2,64,4,1536]{3,2,0,1:T(4,128)S(1)} async-done(((f32[2,64,4,1536]{3,2,0,1:T(4,128)}), f32[2,64,4,1536]{3,2,0,1:T(4,128)S(1)}, u32[]{:S(2)}, u32[]{:S(2)}) %all-to-all-start.1) | async-done | bytes 3145760 | tf_op jit(solution)/shard_map/all_to_all | solution.py:128
  157.7 2.9 copy.77
  160.6 5.1 %convolution_bitcast_fusion.1 = f32[2,2,128,1536]{2,3,0,1:T(8,128)S(1)} fusion(f32[2,2,128,1536,1]{3,1,2,0,4:T(2,128)S(1)} %bitcast.149, f32[1,128,2,128]{3,1,2,0:T(8,128)S(1)} %get-tuple-element.41, f32[1,128,2,128]{3,1,2,0:T(8,128)S(1)} %get-tuple-element.40), kind=kOutput, calls=%fused_computation.1 | convolution fusion | flops 2415984640 | bytes 6553600 | tf_op jit(solution)/shard_map/ascb,ckbh->aksh/dot_general | solution.py:89
  165.8 0.3 multiply_subtract_fusion.1
  166.1 0.6 copy-done.3
  166.7 2.8 convolution_bitcast_fusion
  169.5 0.3 multiply_subtract_fusion
  170.0 3.6 %copy.83 = f32[2,2,128,1536]{3,0,1,2:T(2,128)} copy(f32[2,2,128,1536]{2,3,0,1:T(8,128)S(1)} %pad_maximum_fusion.1) | data formatting | bytes 6291456 | tf_op jit(solution)/shard_map/stack | solution.py:107
  173.6 3.8 %all-to-all-start.2 = ((f32[2,2,128,1536]{3,0,1,2:T(2,128)}), f32[2,2,128,1536]{3,0,1,2:T(2,128)S(1)}, u32[]{:S(2)}, u32[]{:S(2)}) async-start(f32[2,2,128,1536]{3,0,1,2:T(2,128)} %copy.83), calls=%async_computation.2 | async-start | bytes 6291456 | tf_op jit(solution)/shard_map/all_to_all | solution.py:141
  177.4 4.3 %convert_reduce_fusion = f32[128,1536]{1,0:T(8,128)} fusion(bf16[128,1,1536]{2,1,0:T(2,128)(2,1)} %copy-done), kind=kLoop, calls=%fused_computation.60 | loop fusion | flops 196608 | bytes 1179648 | tf_op jit(solution)/shard_map/convert_element_type | solution.py:122
  181.7 2.3 reshape.564
  184.0 64.7 %all-to-all-done.2 = f32[2,2,128,1536]{3,0,1,2:T(2,128)S(1)} async-done(((f32[2,2,128,1536]{3,0,1,2:T(2,128)}), f32[2,2,128,1536]{3,0,1,2:T(2,128)S(1)}, u32[]{:S(2)}, u32[]{:S(2)}) %all-to-all-start.2) | async-done | bytes 3145760 | tf_op jit(solution)/shard_map/all_to_all | solution.py:141
  248.7 1.2 copy.85
  249.9 1.0 copy.98
  250.9 2.4 copy.86
  253.3 6.9 %fusion.32 = bf16[32,4,1536]{2,0,1:T(8,128)(2,1)S(1)} fusion(f32[32,4,1536]{2,1,0:T(4,128)} %reshape.564, f32[4,1536,128]{2,1,0:T(8,128)} %bitcast.154, f32[1536]{0:T(1024)S(1)} %copy-done.6, f32[32,64]{1,0:T(8,128)S(1)} %get-tuple-element.64, f32[32,64]{1,0:T(8,128)S(1)} %get-tuple-element.65), kind=kOutput, calls=%fused_computation.53 | convolution fusion | flops 315363328 | bytes 4347904 | tf_op jit(solution)/shard_map/dot_general | solution.py:142
  260.2 0.3 copy.88
  260.5 17.1 %all_to_all.51 = bf16[32,4,1536]{2,1,0:T(4,128)(2,1)S(1)} all-to-all(bf16[32,4,1536]{2,1,0:T(4,128)(2,1)S(1)} %copy.88), channel_id=1, replica_groups=mesh['groups'=1,'seq'=32] {'seq'}, dimensions={0} | all-to-all | bytes 786432 | tf_op jit(solution)/shard_map/all_to_all | solution.py:148
  277.7 5.1 %fusion.143 = f32[128,3072]{1,0:T(8,128)S(1)} fusion(bf16[128,1536]{1,0:T(8,128)(2,1)S(1)} %squeeze.31, bf16[1536,3072]{1,0:T(8,128)(2,1)} %all-gather.2.cloned.1.call-done), kind=kOutput, calls=%fused_computation.245 | convolution fusion | flops 1207959552 | bytes 11403264 | tf_op jit(solution)/shard_map/dot_general | solution.py:149
  282.8 1.0 fusion.43
  (39 shorter events, 2.4 us)
Async XLA Ops:
  8.7 12.5 %copy-start.4 = (f32[2,64]{1,0:T(2,128)S(1)}, f32[2,64]{1,0:T(2,128)}, u32[]{:S(2)}) copy-start(f32[2,64]{1,0:T(2,128)} %param.8) | copy-start | bytes 1540
  12.7 20.6 %all-to-all-start = ((bf16[32,2,3072]{2,1,0:T(2,128)(2,1)}), bf16[32,2,3072]{2,1,0:T(2,128)(2,1)S(1)}, u32[]{:S(2)}, u32[]{:S(2)}) async-start(bf16[32,2,3072]{2,1,0:T(2,128)(2,1)} %reshape.574), calls=%async_computation | async-start | bytes 786432 | tf_op jit(solution)/shard_map/all_to_all | solution.py:119
  20.0 257.7 %all-gather.2.cloned.1.call-start = ((), (), s32[]{:S(2)}) async-start(), calls=%async_computation.4 | async-start | bytes 9732096 | tf_op jit(solution)/shard_map/all_gather | solution.py:151
  33.6 4.0 %copy-start = (bf16[128,1,1536]{2,1,0:T(2,128)(2,1)}, bf16[128,1,1536]{2,1,0:T(2,128)(2,1)S(1)}, u32[]{:S(2)}) copy-start(bf16[128,1,1536]{2,1,0:T(2,128)(2,1)S(1)} %reshape.575) | copy-start | bytes 1179652
  45.7 3.2 %copy-start.5 = (f32[2,64]{1,0:T(2,128)S(1)}, f32[2,64]{1,0:T(2,128)}, u32[]{:S(2)}) copy-start(f32[2,64]{1,0:T(2,128)} %param.9) | copy-start | bytes 1540
  45.7 112.0 %all-to-all-start.1 = ((f32[2,64,4,1536]{3,2,0,1:T(4,128)}), f32[2,64,4,1536]{3,2,0,1:T(4,128)S(1)}, u32[]{:S(2)}, u32[]{:S(2)}) async-start(f32[2,64,4,1536]{3,2,0,1:T(4,128)} %pad_maximum_fusion), calls=%async_computation.1 | async-start | bytes 6291456 | tf_op jit(solution)/shard_map/all_to_all | solution.py:128
  160.6 5.1 %copy-start.1 = (f32[1,2,128,1536]{2,3,0,1:T(8,128)S(1)}, f32[1,2,128,1536]{2,3,0,1:T(8,128)}, u32[]{:S(2)}) copy-start(f32[1,2,128,1536]{2,3,0,1:T(8,128)} %copy.80) | copy-start | bytes 4718596
  160.6 5.1 %copy-start.2 = (f32[1,2,128,1536]{2,3,0,1:T(8,128)S(1)}, f32[1,2,128,1536]{2,3,0,1:T(8,128)}, u32[]{:S(2)}) copy-start(f32[1,2,128,1536]{2,3,0,1:T(8,128)} %copy.79) | copy-start | bytes 4718596
  165.7 0.9 copy-start.3
  173.6 75.1 %all-to-all-start.2 = ((f32[2,2,128,1536]{3,0,1,2:T(2,128)}), f32[2,2,128,1536]{3,0,1,2:T(2,128)S(1)}, u32[]{:S(2)}, u32[]{:S(2)}) async-start(f32[2,2,128,1536]{3,0,1,2:T(2,128)} %copy.83), calls=%async_computation.2 | async-start | bytes 6291456 | tf_op jit(solution)/shard_map/all_to_all | solution.py:141
  250.9 2.4 copy-start.6
Sparse Core Ops, SparseCore 0:
  23.7 128.8 all-gather.1
where the time goes:
time: 295 us; the launch traced here: 291 us
  waiting for transfers between devices  164 us (56%)
  local copies, waits for them, and re-layouts  31.4 us (11%)
  matrix products  29.7 us (10%)
  other arithmetic  20.6 us (7%)
  blocking collectives  17.1 us (6%)
  starting transfers between devices  14.5 us (5%)
  between operations  14 us (5%)
    all_to_all x1, waiting for transfers between devices, shards(): lax.all_to_all(spread, 'seq', split_axis=1, concat_axis=2, tiled=True)  86.3 us
    all_to_all x1, waiting for transfers between devices, shards(): lax.all_to_all(inverse, 'seq', split_axis=2, concat_axis=1, tiled=True)  64.7 us
    all_to_all x1, blocking collectives, shards(): lax.all_to_all(activation, 'seq', split_axis=0, concat_axis=1, tiled=True)  17.1 us
    all_to_all x1, waiting for transfers between devices, shards(): lax.all_to_all(tokens[None], 'seq', split_axis=1, concat_axis=0, tiled=True)  12.1 us
    dot_general x4, matrix products, response(): summed = jnp.dot(cauchy_left, matrix, precision=PRECISE)  8.33 us
    dot_general x2, matrix products, transform(): jnp.einsum('ascb,ckbh->aksh', dft_table_of(length, direction), signal, pr...  7.88 us
    all_to_all x1, starting transfers between devices, shards(): lax.all_to_all(tokens[None], 'seq', split_axis=1, concat_axis=0, tiled=True)  7.33 us
    dot_general x1, matrix products, shards(): jnp.dot(inverse_table, returned.reshape(4 * seq_count, per_device * chann...  6.92 us
  transfers between devices with their start and end apart: 4, of which 3 were waited for; matrix products, arithmetic and copies ran while one was open for 24% of the time, Pallas kernels for 0%

commit v1 on v0

v1 whole, which is shorter than its diff:
```python
import functools
import math

import jax
import jax.numpy as jnp
import numpy as np
from jax import lax
from jax.experimental import pallas as pl
from jax.experimental.pallas import tpu as pltpu
from jax.sharding import PartitionSpec as P

F32 = jnp.float32
BF16 = jnp.bfloat16


def padded(count):
    return -(-count // 8) * 8


def group_of(count, most):
    return max(g for g in range(1, most + 1) if count % g == 0)


def half_angles(seq_count, tok_rows):
    full_len = 2 * seq_count * tok_rows
    freq = np.arange(seq_count + 1)[:, None] + 2 * seq_count * np.arange(tok_rows)[None, :]
    wrapped = np.where(freq > full_len // 2, freq - full_len, freq).astype(np.float32)
    half = wrapped * np.float32(-2.0 * math.pi / full_len) * np.float32(0.5)
    half = half.astype(np.float64)
    weight = np.full((seq_count + 1, 1), 2.0)
    weight[0] = weight[-1] = 1.0
    weight = np.broadcast_to(weight / (2.0 * full_len), half.shape)
    return np.stack([np.cos(half), np.sin(half), weight]).astype(np.float32)


def split_table(table):
    high = table.astype(jnp.bfloat16).astype(np.float64)
    return high.astype(np.float32), (table - high).astype(np.float32)


def conv_tables(seq_count, tok_rows):
    pairs = seq_count + 1
    rows = padded(pairs)
    full_len = 2 * seq_count * tok_rows
    outer = 2.0 * np.pi * np.outer(np.arange(pairs), np.arange(seq_count)) / (2 * seq_count)
    first = np.zeros((2 * rows, seq_count))
    first[:pairs] = np.cos(outer)
    first[rows : rows + pairs] = -np.sin(outer)
    first = np.concatenate(split_table(first), 1)
    last = np.zeros((seq_count, 2 * rows))
    last[:, :pairs] = np.cos(outer).T
    last[:, rows : rows + pairs] = -np.sin(outer).T
    turn = 2.0 * np.pi * np.outer(np.arange(pairs), np.arange(tok_rows)) / full_len
    twiddle = np.zeros((2, rows, tok_rows))
    twiddle[0, :pairs] = np.cos(turn)
    twiddle[1, :pairs] = np.sin(turn)
    inner = 2.0 * np.pi * np.outer(np.arange(tok_rows), np.arange(tok_rows)) / tok_rows
    cosine, sine = np.cos(inner), np.sin(inner)
    forward = np.block([[cosine, -sine], [sine, cosine]])
    inverse = np.block([[cosine, sine], [-sine, cosine]])
    return (
        jnp.asarray(first, BF16),
        jnp.asarray(twiddle, F32),
        jnp.asarray(forward, BF16),
        jnp.asarray(inverse, BF16),
        jnp.asarray(last, BF16),
    )


def thirds(value):
    high = value.astype(BF16)
    rest = value - high.astype(F32)
    middle = rest.astype(BF16)
    low = (rest - middle.astype(F32)).astype(BF16)
    return high, middle, low


def response_kernel(chans, group, width, tab_ref, rates_ref, left_ref, out_ref):
    cos_half = tab_ref[0, 0:1, :]
    sin_half = tab_ref[0, 1:2, :]
    weight = tab_ref[0, 2:3, :]
    cos_two = jnp.concatenate([cos_half, cos_half], 1)
    sin_two = jnp.concatenate([sin_half, -sin_half], 1)
    decay = -rates_ref[:, 0:1]
    spin = rates_ref[:, 1:2]
    power = rates_ref[:, 2:3]
    real_part = cos_two * decay
    imag_part = -(2.0 * sin_two + cos_two * spin)
    inv_norm = 1.0 / (real_part * real_part + imag_part * imag_part)
    v_real = real_part * inv_norm
    v_imag = -imag_part * inv_norm
    pp_real = jnp.sum(v_real * power, axis=0, keepdims=True)
    pp_imag = jnp.sum(v_imag * power, axis=0, keepdims=True)
    den_real = 1.0 + cos_two * pp_real
    den_imag = cos_two * pp_imag
    den_inv = cos_two / (den_real * den_real + den_imag * den_imag)
    d_real = den_real * den_inv
    d_imag = -den_imag * den_inv
    v_high, v_mid, v_low = thirds(jnp.concatenate([v_real, v_imag], 0))
    l_high, l_mid, l_low = thirds(left_ref[...])
    right_a = jnp.concatenate([v_high, v_mid], 0)
    right_b = jnp.concatenate([v_low, v_high], 0)

    def sums(index):
        rows = slice(index * chans, (index + 1) * chans)
        high, mid, low = l_high[rows], l_mid[rows], l_low[rows]
        return (
            jnp.dot(jnp.concatenate([high, low], 1), right_b, preferred_element_type=F32)
            + jnp.dot(jnp.concatenate([mid, mid], 1), right_a, preferred_element_type=F32)
            + jnp.dot(jnp.concatenate([high, high], 1), right_a, preferred_element_type=F32)
        )

    cb_real, cb_imag, cp_real, cp_imag, pb_real, pb_imag = [sums(i) for i in range(6)]
    num_real = cp_real * pb_real - cp_imag * pb_imag
    num_imag = cp_real * pb_imag + cp_imag * pb_real
    q_real = cb_real - (num_real * d_real - num_imag * d_imag)
    q_imag = cb_imag - (num_real * d_imag + num_imag * d_real)
    half = group * width
    b_real = (q_real[:, :half] + q_real[:, half:]) * weight
    b_imag = (q_imag[:, :half] - q_imag[:, half:]) * weight
    s_real = b_real * cos_half + b_imag * sin_half
    s_imag = b_imag * cos_half - b_real * sin_half
    for g in range(group):
        cols = slice(g * width, (g + 1) * width)
        out_ref[g, :, :width] = s_real[:, cols]
        out_ref[g, :, width:] = s_imag[:, cols]


def half_spectrum(tables, rates, left, chans, width):
    pairs = tables.shape[1]
    group = group_of(pairs, 6)
    steps = pairs // group
    states = rates.shape[0]
    tables = tables.reshape(3, steps, group * width).transpose(1, 0, 2)
    return pl.pallas_call(
        functools.partial(response_kernel, chans, group, width),
        grid=(steps,),
        in_specs=[
            pl.BlockSpec((1, 3, group * width), lambda i: (i, 0, 0)),
            pl.BlockSpec((states, 3), lambda i: (0, 0)),
            pl.BlockSpec((6 * chans, 2 * states), lambda i: (0, 0)),
        ],
        out_specs=pl.BlockSpec((group, chans, 2 * width), lambda i: (i, 0, 0)),
        out_shape=jax.ShapeDtypeStruct((pairs, chans, 2 * width), F32),
        cost_estimate=pl.CostEstimate(
            flops=pairs * width * chans * states * 48, bytes_accessed=1 << 21, transcendentals=0
        ),
        name="response",
    )(tables, rates, left)


def conv_kernel(
    seq_count, chans, width, per_loop,
    x_ref, s_ref, skip_ref, first_ref, tw_ref, forward_ref, inverse_ref, last_ref,
    out_ref, xf, ar, ai,
):
    pairs = seq_count + 1
    rows = padded(pairs)
    bundle = 4
    for s in range(seq_count):
        xf[s * chans : (s + 1) * chans, :] = x_ref[s].astype(F32)
    tw_cos, tw_sin = tw_ref[0], tw_ref[1]
    for base in range(0, chans, bundle):
        parts = [xf[pl.ds(base + j, seq_count, stride=chans), :] for j in range(bundle)]
        right = jnp.concatenate(parts, 1).astype(BF16)
        right = jnp.concatenate([right, right], 0)
        got = jnp.dot(first_ref[...], right, preferred_element_type=F32)
        for j in range(bundle):
            cols = slice(j * width, (j + 1) * width)
            real, imag = got[:rows, cols], got[rows:, cols]
            ar[pl.ds(base + j, rows, stride=chans), :] = real * tw_cos + imag * tw_sin
            ai[pl.ds(base + j, rows, stride=chans), :] = imag * tw_cos - real * tw_sin

    span = per_loop * chans

    def step(index, carry):
        at = pl.ds(pl.multiple_of(index * span, 8), span)
        left = jnp.concatenate([ar[at, :], ai[at, :]], 1).astype(BF16)
        spec = jnp.dot(left, forward_ref[...], preferred_element_type=F32)
        filt = s_ref[pl.ds(index * per_loop, per_loop)].reshape(span, 2 * width)
        x_r, x_i = spec[:, :width], spec[:, width:]
        f_r, f_i = filt[:, :width], filt[:, width:]
        prod = jnp.concatenate([x_r * f_r - x_i * f_i, x_r * f_i + x_i * f_r], 1)
        back = jnp.dot(prod.astype(BF16), inverse_ref[...], preferred_element_type=F32)
        ar[at, :] = back[:, :width]
        ai[at, :] = back[:, width:]
        return carry

    lax.fori_loop(0, pairs // per_loop, step, 0)

    for base in range(0, chans, bundle):
        parts = []
        for j in range(bundle):
            real = ar[pl.ds(base + j, rows, stride=chans), :]
            imag = ai[pl.ds(base + j, rows, stride=chans), :]
            parts.append(
                jnp.concatenate(
                    [real * tw_cos - imag * tw_sin, imag * tw_cos + real * tw_sin], 0
                )
            )
        right = jnp.concatenate(parts, 1).astype(BF16)
        got = jnp.dot(last_ref[...], right, preferred_element_type=F32)
        for j in range(bundle):
            at = pl.ds(base + j, seq_count, stride=chans)
            skip = skip_ref[base + j : base + j + 1, :]
            xf[at, :] = got[:, j * width : (j + 1) * width] + skip * xf[at, :]
    for s in range(seq_count):
        pre = xf[s * chans : (s + 1) * chans, :]
        act = 0.5 * pre * (1.0 + lax.erf(pre * math.sqrt(0.5)))
        out_ref[s] = act.astype(BF16)


def filtered(columns, spectrum, skip, seq_count, chans, width):
    pairs = seq_count + 1
    tables = conv_tables(seq_count, width)
    per_loop = group_of(pairs, 13)
    return pl.pallas_call(
        functools.partial(conv_kernel, seq_count, chans, width, per_loop),
        out_shape=jax.ShapeDtypeStruct((seq_count, chans, width), BF16),
        scratch_shapes=[
            pltpu.VMEM((seq_count * chans, width), F32),
            pltpu.VMEM((padded(pairs) * chans, width), F32),
            pltpu.VMEM((padded(pairs) * chans, width), F32),
        ],
        cost_estimate=pl.CostEstimate(
            flops=1 << 29, bytes_accessed=1 << 21, transcendentals=1 << 18
        ),
        name="conv",
    )(columns, spectrum, skip, *tables)


def complex_mul(first, second):
    return (
        first[0] * second[0] - first[1] * second[1],
        first[0] * second[1] + first[1] * second[0],
    )


def left_matrix(coupling, in_own, out_own):
    low = (coupling[0][:, None], coupling[1][:, None])
    low_conj = (low[0], -low[1])
    blocks = []
    for first, second in ((out_own, in_own), (out_own, low), (low_conj, in_own)):
        real, imag = complex_mul(first, second)
        blocks.append(jnp.concatenate([real, -imag], 0).T)
        blocks.append(jnp.concatenate([imag, real], 0).T)
    return jnp.concatenate(blocks, 0)


def shards(tokens, state_rates, coupling, in_proj, out_proj, skip_gain, mix_weight):
    seq_count = lax.axis_size("seq")
    place = lax.axis_index("seq")
    width, channels = tokens.shape
    chans = channels // seq_count
    columns = tokens.T.reshape(seq_count, chans, width)
    columns = lax.all_to_all(columns, "seq", 0, 0)
    in_own = lax.dynamic_slice_in_dim(in_proj, place * chans, chans, 2)
    out_own = lax.dynamic_slice_in_dim(out_proj, place * chans, chans, 2)
    skip = lax.dynamic_slice_in_dim(skip_gain, place * chans, chans, 0)[:, None]
    left = left_matrix(coupling, in_own, out_own)
    power = coupling[0] * coupling[0] + coupling[1] * coupling[1]
    rates = jnp.stack([state_rates[0], state_rates[1], power], 1)
    tables = jnp.asarray(half_angles(seq_count, width))
    spectrum = half_spectrum(tables, rates, left, chans, width)
    activation = filtered(columns, spectrum, skip, seq_count, chans, width)
    act = lax.all_to_all(activation, "seq", 0, 0).reshape(channels, width)
    weight = lax.all_gather(mix_weight, "seq", axis=0, tiled=True)
    projected = lax.dot_general(act, weight, (((0,), (0,)), ((), ())), preferred_element_type=F32)
    return (projected[:, :channels] * jax.nn.sigmoid(projected[:, channels:])).astype(BF16)


def solution(mesh):
    placed = (P(("groups", "seq"), None), P(), P(), P(), P(), P(), P("seq", None))
    return jax.shard_map(
        shards, mesh=mesh, in_specs=placed, out_specs=P(("groups", "seq"), None), check_vma=False
    )
```

time: 295 us -> 116 us (0.39); the launches traced: 291 us -> 116 us
  waiting for transfers between devices: 164 us -> 34.4 us
  matrix products: 29.7 us -> 5.1 us
  Pallas kernels: 0 us -> 24.6 us
  local copies, waits for them, and re-layouts: 31.4 us -> 6.94 us
  other arithmetic: 20.6 us -> 2.91 us
  starting transfers between devices: 14.5 us -> 7.33 us
  blocking collectives: 17.1 us -> 21.1 us
    all_to_all x3 -> x1, waiting for transfers between devices: 163 us -> 0.01 us  [shards(): columns = lax.all_to_all(columns, 'seq', 0, 0)]
    all_gather x1, waiting for transfers between devices: 0.02 us -> 33.7 us  [shards(): weight = lax.all_gather(mix_weight, 'seq', axis=0, tiled=True)]
    pallas_call x0 -> x2, Pallas kernels: none -> 24.6 us  [the longest x1 18.8 us: half_spectrum(): pl.pallas_call(functools.partial(response_kernel, chans, group, width), g...]
    dot_general x9 -> x1, matrix products: 29.7 us -> 5.1 us  [shards(): lax.dot_general(act, weight, (((0,), (0,)), ((), ())), preferred_element_...]
    all_to_all x3 -> x1, starting transfers between devices: 14.2 us -> 7.33 us  [shards(): columns = lax.all_to_all(columns, 'seq', 0, 0)]
    all_to_all x3 -> x0, local copies, waits for them, and re-layouts: 6.34 us -> none  [the longest x1 2.89 us: shards(): lax.all_to_all(spread, 'seq', split_axis=1, concat_axis=2, tiled=True)]
    reshape x3 -> x0, local copies, waits for them, and re-layouts: 6.34 us -> none  [the longest x1 3.05 us: shards(): kernel_imag.reshape(2, tok_rows, channels)]
    convert_element_type x1 -> x0, other arithmetic: 4.25 us -> none  [shards(): columns.astype(jnp.float32).reshape(seq_count, per_device * channels)]
  transfers between devices with their start and end apart: 4 -> 2, of which waited for: 3 -> 1; matrix products, arithmetic and copies ran while one was open for 24% -> 6% of each run, Pallas kernels for 0% -> 21%
where the time goes in v1:
time: 116 us
  waiting for transfers between devices  34.4 us (30%)
  Pallas kernels  24.6 us (21%)
  blocking collectives  21.1 us (18%)
  between operations  13.4 us (12%)
  starting transfers between devices  7.33 us (6%)
  local copies, waits for them, and re-layouts  6.94 us (6%)
  matrix products  5.1 us (4%)
  other arithmetic  2.91 us (3%)
    all_gather x1, waiting for transfers between devices, shards(): weight = lax.all_gather(mix_weight, 'seq', axis=0, tiled=True)  33.7 us
    all_to_all x1, blocking collectives, shards(): act = lax.all_to_all(activation, 'seq', 0, 0).reshape(channels, width)  21.1 us
    pallas_call x1, Pallas kernels, half_spectrum(): pl.pallas_call(functools.partial(response_kernel, chans, group, width), g...  18.8 us
    all_to_all x1, starting transfers between devices, shards(): columns = lax.all_to_all(columns, 'seq', 0, 0)  7.33 us
    pallas_call x1, Pallas kernels, filtered(): pl.pallas_call(functools.partial(conv_kernel, seq_count, chans, width, pe...  5.8 us
    dot_general x1, matrix products, shards(): lax.dot_general(act, weight, (((0,), (0,)), ((), ())), preferred_element_...  5.1 us
  transfers between devices with their start and end apart: 2, of which 1 were waited for; matrix products, arithmetic and copies ran while one was open for 6% of the time, Pallas kernels for 21%

profile of v1, /device:TPU:0, one launch (start us, length us, event | category | flops | bytes accessed | tf_op | source)
XLA Modules:
  0.0 115.9 jit_solution(12398151674478704781)
XLA Ops:
  6.5 0.0 copy-start
  6.5 0.0 all-gather.2.cloned.1.call-start
  6.5 0.7 all-gather.2.cloned.1.call-update
  7.3 1.9 %copy.21 = bf16[1536,128]{1,0:T(8,128)(2,1)} copy(bf16[1536,128]{0,1:T(8,128)(2,1)} %bitcast.96) | data formatting | bytes 786432 | tf_op jit(solution)/shard_map/transpose | solution.py:255
  9.2 7.3 %all-to-all-start = ((bf16[32,48,128]{2,1,0:T(8,128)(2,1)}), bf16[32,48,128]{2,1,0:T(8,128)(2,1)S(1)}, u32[]{:S(2)}, u32[]{:S(2)}) async-start(bf16[32,48,128]{2,1,0:T(8,128)(2,1)} %bitcast.1), calls=%async_computation | async-start | bytes 786432 | tf_op jit(solution)/shard_map/all_to_all | solution.py:256
  16.5 1.0 constant_dynamic-slice_fusion.1
  17.6 0.1 copy.27
  17.6 0.1 copy.29
  17.7 0.1 copy.30
  17.8 0.1 copy.31
  17.9 0.8 slice_bitcast_fusion.2
  18.6 0.8 slice_bitcast_fusion.1
  19.4 0.7 fusion.17
  20.1 0.0 copy-done
  20.1 0.1 dynamic-slice_bitcast_fusion
  20.2 0.7 copy.24.rates_ref
  20.9 0.7 copy.25.skip_ref
  21.6 0.1 fusion.5
  21.7 0.1 fusion.6
  21.8 0.1 fusion.7
  21.9 0.1 fusion.8
  21.9 0.1 fusion.9
  22.0 0.1 fusion.10.left_ref
  22.1 0.0 copy-start.2
  22.1 0.7 copy-done.2
  22.8 18.8 %response.1.s_ref = f32[33,48,256]{2,1,0:T(8,128)} custom-call(f32[11,3,384]{2,1,0:T(4,128)} %constant.32.tab_ref, f32[64,3]{1,0:T(8,128)} %copy.24.rates_ref, f32[288,128]{1,0:T(8,128)} %copy-done.2), custom_call_target="tpu_custom_call" | custom-call | flops 622854144 | bytes 2097152 | tf_op jit(solution)/shard_map/response/pallas_call | solution.py:135
  41.6 0.0 all-to-all-done.x_ref
  41.6 0.0 copy-start.1
  41.6 0.7 copy-done.1
  42.3 5.8 %conv.1 = bf16[32,48,128]{2,1,0:T(8,128)(2,1)} custom-call(bf16[32,48,128]{2,1,0:T(8,128)(2,1)} %copy-done.1, f32[33,48,256]{2,1,0:T(8,128)} %response.1.s_ref, f32[48,1]{1,0:T(8,128)} %copy.25.skip_ref, bf16[80,64]{1,0:T(8,128)(2,1)} %constant.25.clone.first_ref, f32[2,40,128]{2,1,0:T(8,128)} %constant.26.clone.tw_ref, ...), custom_call_target="tpu_custom_call" | custom-call | flops 536870912 | bytes 2097152 | tf_op jit(solution)/shard_map/conv/pallas_call | solution.py:217
  48.1 21.1 %all_to_all.10 = bf16[32,48,128]{2,1,0:T(8,128)(2,1)S(1)} all-to-all(bf16[32,48,128]{2,1,0:T(8,128)(2,1)} %conv.1), channel_id=1, replica_groups=mesh['groups'=1,'seq'=32] {'seq'}, dimensions={0} | all-to-all | bytes 786432 | tf_op jit(solution)/shard_map/all_to_all | solution.py:266
  69.2 33.7 %all-gather.2.cloned.1.call-done = bf16[1536,3072]{1,0:T(8,128)(2,1)} async-done(((bf16[48,3072]{1,0:T(8,128)(2,1)}), bf16[1536,3072]{1,0:T(8,128)(2,1)}) %all-gather.2.cloned.1.call-update) | async-done | bytes 9437200 | tf_op jit(solution)/shard_map/all_gather | solution.py:267
  103.0 5.1 %fusion.24 = f32[128,3072]{1,0:T(8,128)S(1)} fusion(bf16[1536,128]{1,0:T(8,128)(2,1)S(1)} %bitcast.95, bf16[1536,3072]{1,0:T(8,128)(2,1)} %all-gather.2.cloned.1.call-done), kind=kOutput, calls=%fused_computation.51 | convolution fusion | flops 1207959552 | bytes 11403264 | tf_op jit(solution)/shard_map/dot_general | solution.py:268
  108.1 1.0 fusion.4
  (2 shorter events, 0.0 us)
Async XLA Ops:
  6.5 13.6 %copy-start = (f32[1536]{0:T(1024)S(1)}, f32[1536]{0:T(1024)}, u32[]{:S(2)}) copy-start(f32[1536]{0:T(1024)} %param.18) | copy-start | bytes 18436
  6.5 96.4 %all-gather.2.cloned.1.call-start = ((), (), s32[]{:S(2)}) async-start(), calls=%async_computation.2 | async-start | bytes 9732096 | tf_op jit(solution)/shard_map/all_gather | solution.py:267
  9.2 32.4 %all-to-all-start = ((bf16[32,48,128]{2,1,0:T(8,128)(2,1)}), bf16[32,48,128]{2,1,0:T(8,128)(2,1)S(1)}, u32[]{:S(2)}, u32[]{:S(2)}) async-start(bf16[32,48,128]{2,1,0:T(8,128)(2,1)} %bitcast.1), calls=%async_computation | async-start | bytes 786432 | tf_op jit(solution)/shard_map/all_to_all | solution.py:256
  22.1 0.7 copy-start.2
  41.6 0.7 copy-start.1
Sparse Core Ops, SparseCore 0:
  10.2 92.6 all-gather.1

commit v2 on v1

--- a/solution.py
+++ b/solution.py
@@ -7,7 +7,8 @@
 from jax import lax
 from jax.experimental import pallas as pl
 from jax.experimental.pallas import tpu as pltpu
-from jax.sharding import PartitionSpec as P
+from jax.sharding import Mesh, PartitionSpec as P
+
 
 F32 = jnp.float32
 BF16 = jnp.bfloat16
@@ -101,16 +102,17 @@
     right_a = jnp.concatenate([v_high, v_mid], 0)
     right_b = jnp.concatenate([v_low, v_high], 0)
 
-    def sums(index):
-        rows = slice(index * chans, (index + 1) * chans)
-        high, mid, low = l_high[rows], l_mid[rows], l_low[rows]
-        return (
-            jnp.dot(jnp.concatenate([high, low], 1), right_b, preferred_element_type=F32)
-            + jnp.dot(jnp.concatenate([mid, mid], 1), right_a, preferred_element_type=F32)
-            + jnp.dot(jnp.concatenate([high, high], 1), right_a, preferred_element_type=F32)
-        )
-
-    cb_real, cb_imag, cp_real, cp_imag, pb_real, pb_imag = [sums(i) for i in range(6)]
+    left_b = jnp.concatenate([l_high, l_low], 1)
+    left_a = jnp.concatenate(
+        [jnp.concatenate([l_mid, l_mid], 1), jnp.concatenate([l_high, l_high], 1)], 0
+    )
+    part_a = jnp.dot(left_a, right_a, preferred_element_type=F32)
+    part_b = jnp.dot(left_b, right_b, preferred_element_type=F32)
+    total = 6 * chans
+    sums = (part_b + part_a[:total]) + part_a[total:]
+    cb_real, cb_imag, cp_real, cp_imag, pb_real, pb_imag = [
+        sums[i * chans : (i + 1) * chans] for i in range(6)
+    ]
     num_real = cp_real * pb_real - cp_imag * pb_imag
     num_imag = cp_real * pb_imag + cp_imag * pb_real
     q_real = cb_real - (num_real * d_real - num_imag * d_imag)
@@ -126,12 +128,12 @@
         out_ref[g, :, width:] = s_imag[:, cols]
 
 
-def half_spectrum(tables, rates, left, chans, width):
+def half_spectrum(tables, rates, left, chans, width, group):
     pairs = tables.shape[1]
-    group = group_of(pairs, 6)
     steps = pairs // group
     states = rates.shape[0]
     tables = tables.reshape(3, steps, group * width).transpose(1, 0, 2)
+    tables = jnp.asarray(tables)
     return pl.pallas_call(
         functools.partial(response_kernel, chans, group, width),
         grid=(steps,),
@@ -150,8 +152,8 @@
 
 
 def conv_kernel(
-    seq_count, chans, width, per_loop,
-    x_ref, s_ref, skip_ref, first_ref, tw_ref, forward_ref, inverse_ref, last_ref,
+    seq_count, chans, width,
+    x_ref, s_ref, t_ref, skip_ref, first_ref, tw_ref, forward_ref, inverse_ref, last_ref,
     out_ref, xf, ar, ai,
 ):
     pairs = seq_count + 1
@@ -171,22 +173,26 @@
             ar[pl.ds(base + j, rows, stride=chans), :] = real * tw_cos + imag * tw_sin
             ai[pl.ds(base + j, rows, stride=chans), :] = imag * tw_cos - real * tw_sin
 
-    span = per_loop * chans
-
-    def step(index, carry):
-        at = pl.ds(pl.multiple_of(index * span, 8), span)
-        left = jnp.concatenate([ar[at, :], ai[at, :]], 1).astype(BF16)
-        spec = jnp.dot(left, forward_ref[...], preferred_element_type=F32)
-        filt = s_ref[pl.ds(index * per_loop, per_loop)].reshape(span, 2 * width)
-        x_r, x_i = spec[:, :width], spec[:, width:]
-        f_r, f_i = filt[:, :width], filt[:, width:]
-        prod = jnp.concatenate([x_r * f_r - x_i * f_i, x_r * f_i + x_i * f_r], 1)
-        back = jnp.dot(prod.astype(BF16), inverse_ref[...], preferred_element_type=F32)
-        ar[at, :] = back[:, :width]
-        ai[at, :] = back[:, width:]
-        return carry
-
-    lax.fori_loop(0, pairs // per_loop, step, 0)
+    def filter_rows(source, start, per_loop):
+        span = per_loop * chans
+
+        def step(index, carry):
+            at = pl.ds(pl.multiple_of(start * chans + index * span, 8), span)
+            left = jnp.concatenate([ar[at, :], ai[at, :]], 1).astype(BF16)
+            spec = jnp.dot(left, forward_ref[...], preferred_element_type=F32)
+            filt = source[pl.ds(index * per_loop, per_loop)].reshape(span, 2 * width)
+            x_r, x_i = spec[:, :width], spec[:, width:]
+            f_r, f_i = filt[:, :width], filt[:, width:]
+            prod = jnp.concatenate([x_r * f_r - x_i * f_i, x_r * f_i + x_i * f_r], 1)
+            back = jnp.dot(prod.astype(BF16), inverse_ref[...], preferred_element_type=F32)
+            ar[at, :] = back[:, :width]
+            ai[at, :] = back[:, width:]
+            return carry
+
+        lax.fori_loop(0, source.shape[0] // per_loop, step, 0)
+
+    filter_rows(s_ref, 0, group_of(s_ref.shape[0], 13))
+    filter_rows(t_ref, s_ref.shape[0], group_of(t_ref.shape[0], 13))
 
     for base in range(0, chans, bundle):
         parts = []
@@ -207,16 +213,15 @@
     for s in range(seq_count):
         pre = xf[s * chans : (s + 1) * chans, :]
         act = 0.5 * pre * (1.0 + lax.erf(pre * math.sqrt(0.5)))
-        out_ref[s] = act.astype(BF16)
+        out_ref[s // 2, :, (s % 2) * width : (s % 2 + 1) * width] = act.astype(BF16)
 
 
 def filtered(columns, spectrum, skip, seq_count, chans, width):
     pairs = seq_count + 1
     tables = conv_tables(seq_count, width)
-    per_loop = group_of(pairs, 13)
     return pl.pallas_call(
-        functools.partial(conv_kernel, seq_count, chans, width, per_loop),
-        out_shape=jax.ShapeDtypeStruct((seq_count, chans, width), BF16),
+        functools.partial(conv_kernel, seq_count, chans, width),
+        out_shape=jax.ShapeDtypeStruct((seq_count // 2, chans, 2 * width), BF16),
         scratch_shapes=[
             pltpu.VMEM((seq_count * chans, width), F32),
             pltpu.VMEM((padded(pairs) * chans, width), F32),
@@ -226,7 +231,7 @@
             flops=1 << 29, bytes_accessed=1 << 21, transcendentals=1 << 18
         ),
         name="conv",
-    )(columns, spectrum, skip, *tables)
+    )(columns, *spectrum, skip, *tables)
 
 
 def complex_mul(first, second):
@@ -247,30 +252,151 @@
     return jnp.concatenate(blocks, 0)
 
 
+AXES = ("chip", "core")
+
+
+def weight_pieces(mix_weight, chip_count):
+    chip, core = lax.axis_index("chip"), lax.axis_index("core")
+    if chip_count != 16:
+        whole = lax.all_gather(mix_weight, "chip", axis=0)
+        return [whole], jnp.arange(chip_count, dtype=jnp.int32)
+    spots = [(z, y, x, c) for z in range(4) for y in range(2) for x in range(2) for c in range(2)]
+
+    def moved(value, target):
+        number = lambda z, y, x, c: ((z * 2 + y) * 2 + x) * 2 + c
+        pairs = [(number(*spot), number(*target(*spot))) for spot in spots]
+        return lax.ppermute(value, AXES, pairs)
+
+    def near(z, y, x, c):
+        return (z, y, 1 - x, c) if c == 0 else (z, 1 - y, x, c)
+
+    def far(z, y, x, c):
+        return (z, 1 - y, x, c) if c == 0 else (z, y, 1 - x, c)
+
+    pieces, raised = [], {0: mix_weight}
+    for offset, source, lift in ((0, 0, 0), (1, 0, 1), (3, 0, 3), (2, 1, 1)):
+        if offset:
+            raised[offset] = moved(
+                raised[source], lambda z, y, x, c: ((z + lift) % 4, y, x, c)
+            )
+        block = raised[offset]
+        beside = moved(block, near)
+        across = moved(block, far)
+        corner = moved(beside, far)
+        pieces += [value[None] for value in (block, beside, across, corner)]
+    slot = jnp.arange(16, dtype=jnp.int32)
+    kind = slot % 4
+    twist = jnp.where(core == 0, kind, jnp.where((kind == 1) | (kind == 2), 3 - kind, kind))
+    offset = jnp.where(slot < 8, slot // 4, 5 - slot // 4)
+    order = ((chip // 4 + 4 - offset) % 4) * 4 + jnp.bitwise_xor(chip % 4, twist)
+    return pieces, order.astype(jnp.int32)
+
+
+def mix_kernel(width, order_ref, act_ref, *refs):
+    *piece_refs, theirs_ref, ours_ref, left = refs
+    chips, chans, _ = act_ref.shape
+    core = order_ref[chips]
+    theirs = pl.multiple_of((1 - core) * width, width)
+    ours = pl.multiple_of(core * width, width)
+    for j in range(chips):
+        rows = slice(j * chans, (j + 1) * chans)
+        left[rows, :width] = act_ref[order_ref[j], :, pl.ds(theirs, width)]
+        left[rows, width:] = act_ref[order_ref[j], :, pl.ds(ours, width)]
+    tokens = left[...].T
+    tile = 512
+    for col in range(0, theirs_ref.shape[1], tile):
+        parts = []
+        for piece in piece_refs:
+            rows = piece.shape[0] * piece.shape[1]
+            parts.append(piece[:, :, col : col + tile].reshape(rows, tile))
+        block = jnp.concatenate(parts, 0)
+        total = jnp.dot(tokens, block, preferred_element_type=F32)
+        theirs_ref[:, col : col + tile] = total[:width].astype(BF16)
+        ours_ref[:, col : col + tile] = total[width:]
+
+
+def mixed(act, pieces, order, core, width):
+    chips, chans, both = act.shape
+    cols = pieces[0].shape[-1]
+    table = jnp.where(jnp.arange(chips + 1) < chips, jnp.pad(order, (0, 1)), core)
+    return pl.pallas_call(
+        functools.partial(mix_kernel, width),
+        in_specs=[pl.BlockSpec(memory_space=pltpu.SMEM)]
+        + [pl.BlockSpec(memory_space=pltpu.VMEM)] * (1 + len(pieces)),
+        out_specs=[pl.BlockSpec(memory_space=pltpu.VMEM)] * 2,
+        out_shape=[
+            jax.ShapeDtypeStruct((width, cols), BF16),
+            jax.ShapeDtypeStruct((width, cols), F32),
+        ],
+        scratch_shapes=[pltpu.VMEM((chips * chans, both), BF16)],
+        cost_estimate=pl.CostEstimate(
+            flops=2 * both * chips * chans * cols,
+            bytes_accessed=chips * chans * cols * 2,
+            transcendentals=0,
+        ),
+        name="mix",
+    )(table.astype(jnp.int32), act, *pieces)
+
+
+def finish_kernel(ours_ref, arrived_ref, out_ref):
+    cols = out_ref.shape[1]
+    for col in range(0, cols, 256):
+        at, gate_at = slice(col, col + 256), slice(cols + col, cols + col + 256)
+        value = ours_ref[:, at] + arrived_ref[:, at].astype(F32)
+        gate = ours_ref[:, gate_at] + arrived_ref[:, gate_at].astype(F32)
+        out_ref[:, at] = (value * jax.nn.sigmoid(gate)).astype(BF16)
+
+
+def finished(ours, arrived):
+    rows, cols = ours.shape
+    return pl.pallas_call(
+        finish_kernel,
+        in_specs=[pl.BlockSpec(memory_space=pltpu.VMEM)] * 2,
+        out_specs=pl.BlockSpec(memory_space=pltpu.VMEM),
+        out_shape=jax.ShapeDtypeStruct((rows, cols // 2), BF16),
+        cost_estimate=pl.CostEstimate(
+            flops=rows * cols * 4, bytes_accessed=rows * cols * 7, transcendentals=rows * cols
+        ),
+        name="finish",
+    )(ours, arrived)
+
+
 def shards(tokens, state_rates, coupling, in_proj, out_proj, skip_gain, mix_weight):
-    seq_count = lax.axis_size("seq")
-    place = lax.axis_index("seq")
+    chip_count = lax.axis_size("chip")
+    seq_count = chip_count * lax.axis_size("core")
+    core = lax.axis_index("core")
+    place = lax.axis_index(AXES)
     width, channels = tokens.shape
     chans = channels // seq_count
     columns = tokens.T.reshape(seq_count, chans, width)
-    columns = lax.all_to_all(columns, "seq", 0, 0)
+    columns = lax.all_to_all(columns, AXES, 0, 0)
+    pieces, order = weight_pieces(mix_weight, chip_count)
+    skip = lax.dynamic_slice_in_dim(skip_gain, place * chans, chans, 0)[:, None]
     in_own = lax.dynamic_slice_in_dim(in_proj, place * chans, chans, 2)
     out_own = lax.dynamic_slice_in_dim(out_proj, place * chans, chans, 2)
-    skip = lax.dynamic_slice_in_dim(skip_gain, place * chans, chans, 0)[:, None]
     left = left_matrix(coupling, in_own, out_own)
     power = coupling[0] * coupling[0] + coupling[1] * coupling[1]
     rates = jnp.stack([state_rates[0], state_rates[1], power], 1)
-    tables = jnp.asarray(half_angles(seq_count, width))
-    spectrum = half_spectrum(tables, rates, left, chans, width)
+    tables = half_angles(seq_count, width)
+    pairs = tables.shape[1]
+    group = group_of(pairs, 6)
+    cut = -(-pairs // group // 2) * group
+    spectrum = []
+    for part in (tables[:, :cut], tables[:, cut:]):
+        spectrum.append(half_spectrum(part, rates, left, chans, width, group))
     activation = filtered(columns, spectrum, skip, seq_count, chans, width)
-    act = lax.all_to_all(activation, "seq", 0, 0).reshape(channels, width)
-    weight = lax.all_gather(mix_weight, "seq", axis=0, tiled=True)
-    projected = lax.dot_general(act, weight, (((0,), (0,)), ((), ())), preferred_element_type=F32)
-    return (projected[:, :channels] * jax.nn.sigmoid(projected[:, channels:])).astype(BF16)
+    act = lax.all_to_all(activation, "chip", 0, 0)
+    theirs, ours = mixed(act, pieces, order, core, width)
+    arrived = lax.ppermute(theirs, "core", [(0, 1), (1, 0)])
+    return finished(ours, arrived)
 
 
 def solution(mesh):
-    placed = (P(("groups", "seq"), None), P(), P(), P(), P(), P(), P("seq", None))
+    groups, seq = mesh.shape["groups"], mesh.shape["seq"]
+    chips = Mesh(mesh.devices.reshape(groups, seq // 2, 2), ("groups", *AXES))
+    rows = ("groups", *AXES)
+
+    placed = (P(rows, None), P(), P(), P(), P(), P(), P(AXES, None))
     return jax.shard_map(
-        shards, mesh=mesh, in_specs=placed, out_specs=P(("groups", "seq"), None), check_vma=False
+        shards, mesh=chips, in_specs=placed, out_specs=P(rows, None), check_vma=False
     )

time: 116 us -> 98.7 us (0.85)
  starting transfers between devices: 7.33 us -> 29.6 us
  blocking collectives: 21.1 us -> 0 us
  between operations: 13.4 us -> 0.21 us
  matrix products: 5.1 us -> 0 us
  other arithmetic: 2.91 us -> 1.12 us
    ppermute x0 -> x16, waiting for transfers between devices: none -> 34.6 us  [the longest x15 32.1 us: moved(): return lax.ppermute(value, AXES, pairs)]
    all_gather x1 -> x0, waiting for transfers between devices: 33.7 us -> none  [shards(): weight = lax.all_gather(mix_weight, 'seq', axis=0, tiled=True)]
    ppermute x0 -> x16, starting transfers between devices: none -> 21.2 us  [the longest x15 21.2 us: moved(): return lax.ppermute(value, AXES, pairs)]
    all_to_all x1 -> x0, blocking collectives: 21.1 us -> none  [shards(): act = lax.all_to_all(activation, 'seq', 0, 0).reshape(channels, width)]
    pallas_call x1 -> x3, Pallas kernels: 5.8 us -> 14.1 us  [the longest x1 6.32 us: filtered(): pl.pallas_call(functools.partial(conv_kernel, seq_count, chans, width), o...]
    pallas_call x1 -> x2, Pallas kernels: 18.8 us -> 11.2 us  [half_spectrum(): pl.pallas_call(functools.partial(response_kernel, chans, group, width), g...]
    dot_general x1 -> x0, matrix products: 5.1 us -> none  [shards(): lax.dot_general(act, weight, (((0,), (0,)), ((), ())), preferred_element_...]
    all_to_all x1 -> x2, starting transfers between devices: 7.33 us -> 8.31 us  [the longest x1 4.19 us: shards(): columns = lax.all_to_all(columns, AXES, 0, 0)]
  transfers between devices with their start and end apart: 2 -> 18, of which waited for: 1 -> 8; matrix products, arithmetic and copies ran while one was open for 6% -> 6% of each run, Pallas kernels for 21% -> 18%
where the time goes in v2:
time: 98.7 us; the launch traced here: 98 us
  waiting for transfers between devices  34.6 us (35%)
  starting transfers between devices  29.6 us (30%)
  Pallas kernels  25.4 us (26%)
  local copies, waits for them, and re-layouts  7.08 us (7%)
  other arithmetic  1.12 us (1%)
    ppermute x15, waiting for transfers between devices, moved(): return lax.ppermute(value, AXES, pairs)  32.1 us
    ppermute x15, starting transfers between devices, moved(): return lax.ppermute(value, AXES, pairs)  21.2 us
    pallas_call x2, Pallas kernels, half_spectrum(): pl.pallas_call(functools.partial(response_kernel, chans, group, width), g...  11.2 us
    pallas_call x1, Pallas kernels, filtered(): pl.pallas_call(functools.partial(conv_kernel, seq_count, chans, width), o...  6.32 us
    pallas_call x1, Pallas kernels, mixed(): pl.pallas_call(functools.partial(mix_kernel, width), in_specs=[pl.BlockSp...  5.28 us
    all_to_all x1, starting transfers between devices, shards(): columns = lax.all_to_all(columns, AXES, 0, 0)  4.19 us
    all_to_all x1, starting transfers between devices, shards(): act = lax.all_to_all(activation, 'chip', 0, 0)  4.12 us
    unnamed x38, local copies, waits for them, and re-layouts  2.64 us
  transfers between devices with their start and end apart: 18, of which 8 were waited for; matrix products, arithmetic and copies ran while one was open for 6% of the time, Pallas kernels for 18%

profile of v2, /device:TPU:0, one launch (start us, length us, event | category | flops | bytes accessed | tf_op | source)
XLA Modules:
  0.0 98.0 jit_solution(4055700846802543859)
XLA Ops:
  0.0 3.1 %collective-permute-start.1 = (bf16[48,3072]{1,0:T(8,128)(2,1)}, bf16[48,3072]{1,0:T(8,128)(2,1)S(1)}, u32[]{:S(2)}, u32[]{:S(2)}) collective-permute-start(bf16[48,3072]{1,0:T(8,128)(2,1)} %param.20), channel_id=1, source_target_pairs={{0,4},{1,3},{2,6},{3,1},{4,0},{5,7},{6,2},{7,5},{8,12},{9,11},{10,... | collective-permute-start | bytes 884744 | tf_op jit(solution)/shard_map/ppermute | solution.py:268
  3.1 1.5 %collective-permute-start = (bf16[48,3072]{1,0:T(8,128)(2,1)}, bf16[48,3072]{1,0:T(8,128)(2,1)S(1)}, u32[]{:S(2)}, u32[]{:S(2)}) collective-permute-start(bf16[48,3072]{1,0:T(8,128)(2,1)} %param.20), channel_id=1, source_target_pairs={{0,2},{1,5},{2,0},{3,7},{4,6},{5,1},{6,4},{7,3},{8,10},{9,13},{10,... | collective-permute-start | bytes 884744 | tf_op jit(solution)/shard_map/ppermute | solution.py:268
  4.6 3.6 %collective-permute-start.7 = (bf16[48,3072]{1,0:T(8,128)(2,1)}, bf16[48,3072]{1,0:T(8,128)(2,1)S(1)}, u32[]{:S(2)}, u32[]{:S(2)}) collective-permute-start(bf16[48,3072]{1,0:T(8,128)(2,1)} %param.20), channel_id=1, source_target_pairs={{0,24},{1,25},{2,26},{3,27},{4,28},{5,29},{6,30},{7,31},{8,0},{9,1... | collective-permute-start | bytes 884744 | tf_op jit(solution)/shard_map/ppermute | solution.py:268
  8.2 1.9 %copy.22 = bf16[1536,128]{1,0:T(8,128)(2,1)} copy(bf16[1536,128]{0,1:T(8,128)(2,1)} %bitcast.108) | data formatting | bytes 786432 | tf_op jit(solution)/shard_map/transpose | solution.py:371
  10.1 4.2 %all-to-all-start = ((bf16[32,48,128]{2,1,0:T(8,128)(2,1)}), bf16[32,48,128]{2,1,0:T(8,128)(2,1)S(1)}, u32[]{:S(2)}, u32[]{:S(2)}) async-start(bf16[32,48,128]{2,1,0:T(8,128)(2,1)} %bitcast.1), calls=%async_computation | async-start | bytes 786432 | tf_op jit(solution)/shard_map/all_to_all | solution.py:372
  14.3 1.0 %constant_dynamic-slice_fusion.1 = (f32[1,64,48]{2,1,0:T(8,128)S(1)}, f32[1,64,48]{2,1,0:T(8,128)S(1)}, f32[1,64,48]{2,1,0:T(8,128)S(1)}, f32[1,64,48]{2,1,0:T(8,128)S(1)}) fusion(f32[2,64,1536]{2,1,0:T(8,128)} %param.18, s32[]{:T(128)S(6)} %select_n.62, s32[]{:T(128)S(6)} %add.68, f32[2,64,1536]{2,1,0:T(8,128)} %param.17), kind=kLoop, calls=%fused_computation.43 | loop fusion | bytes 98312 | tf_op jit(solution)/shard_map/slice | solution.py:239
  15.4 0.1 copy.29
  15.4 0.1 copy.32
  15.5 0.1 copy.31
  15.6 0.1 copy.33
  15.7 0.1 fusion
  15.8 0.1 fusion.1
  15.9 0.1 fusion.2
  16.0 0.1 fusion.3
  16.1 0.1 fusion.4
  16.1 0.1 fusion.5.left_ref
  16.2 6.8 %collective-permute-done.3 = bf16[48,3072]{1,0:T(8,128)(2,1)S(1)} collective-permute-done((bf16[48,3072]{1,0:T(8,128)(2,1)}, bf16[48,3072]{1,0:T(8,128)(2,1)S(1)}, u32[]{:S(2)}, u32[]{:S(2)}) %collective-permute-start.3) | collective-permute-done | bytes 294944 | tf_op jit(solution)/shard_map/ppermute | solution.py:268
  23.0 1.6 %collective-permute-start.11 = (bf16[48,3072]{1,0:T(8,128)(2,1)S(1)}, bf16[48,3072]{1,0:T(8,128)(2,1)S(1)}, u32[]{:S(2)}, u32[]{:S(2)}) collective-permute-start(bf16[48,3072]{1,0:T(8,128)(2,1)S(1)} %collective-permute-done.3), channel_id=1, source_target_pairs={{0,8},{1,9},{2,10},{3,11},{4,12},{5,13},{6,14},{7,15},{8,16},{9,17... | collective-permute-start | bytes 884744 | tf_op jit(solution)/shard_map/ppermute | solution.py:268
  24.6 0.1 dynamic-slice_bitcast_fusion
  24.7 0.7 copy.27.skip_ref
  25.4 0.7 copy.25.rates_ref
  26.1 5.3 %response.3.t_ref = f32[15,48,256]{2,1,0:T(8,128)} custom-call(f32[5,3,384]{2,1,0:T(4,128)} %constant.92.clone.tab_ref, f32[64,3]{1,0:T(8,128)} %copy.25.rates_ref, f32[288,128]{1,0:T(8,128)} %copy-done.14), custom_call_target="tpu_custom_call" | custom-call | flops 283115520 | bytes 2097152 | tf_op jit(solution)/shard_map/response/pallas_call | solution.py:137
  31.3 6.0 %response.2.s_ref = f32[18,48,256]{2,1,0:T(8,128)} custom-call(f32[6,3,384]{2,1,0:T(4,128)} %constant.91.clone.tab_ref, f32[64,3]{1,0:T(8,128)} %copy.25.rates_ref, f32[288,128]{1,0:T(8,128)} %copy-done.14), custom_call_target="tpu_custom_call" | custom-call | flops 339738624 | bytes 2097152 | tf_op jit(solution)/shard_map/response/pallas_call | solution.py:137
  37.3 0.7 copy-done.1
  38.1 6.3 %conv.1 = bf16[16,48,256]{2,1,0:T(8,128)(2,1)} custom-call(bf16[32,48,128]{2,1,0:T(8,128)(2,1)} %copy-done.1, f32[18,48,256]{2,1,0:T(8,128)} %response.2.s_ref, f32[15,48,256]{2,1,0:T(8,128)} %response.3.t_ref, f32[48,1]{1,0:T(8,128)} %copy.27.skip_ref, bf16[80,64]{1,0:T(8,128)(2,1)} %constant.93.clone.first_ref, f32[2,40,128]{2,1,0:T(8,128)} %constant.94.clone.tw_ref, ...), custom_call_target="tpu_custom_call" | custom-call | flops 536870912 | bytes 2097152 | tf_op jit(solution)/shard_map/conv/pallas_call | solution.py:222
  44.4 4.1 %all-to-all-start.1 = ((bf16[16,48,256]{2,1,0:T(8,128)(2,1)}), bf16[16,48,256]{2,1,0:T(8,128)(2,1)S(1)}, u32[]{:S(2)}, u32[]{:S(2)}) async-start(bf16[16,48,256]{2,1,0:T(8,128)(2,1)} %conv.1), calls=%async_computation.1 | async-start | bytes 786432 | tf_op jit(solution)/shard_map/all_to_all | solution.py:388
  48.5 2.0 %collective-permute-start.2 = (bf16[48,3072]{1,0:T(8,128)(2,1)S(1)}, bf16[48,3072]{1,0:T(8,128)(2,1)S(1)}, u32[]{:S(2)}, u32[]{:S(2)}) collective-permute-start(bf16[48,3072]{1,0:T(8,128)(2,1)S(1)} %collective-permute-done), channel_id=1, source_target_pairs={{0,4},{1,3},{2,6},{3,1},{4,0},{5,7},{6,2},{7,5},{8,12},{9,11},{10,... | collective-permute-start | bytes 884744 | tf_op jit(solution)/shard_map/ppermute | solution.py:268
  50.5 0.1 collective-permute-start.9
  50.6 1.9 %collective-permute-start.8 = (bf16[48,3072]{1,0:T(8,128)(2,1)S(1)}, bf16[48,3072]{1,0:T(8,128)(2,1)S(1)}, u32[]{:S(2)}, u32[]{:S(2)}) collective-permute-start(bf16[48,3072]{1,0:T(8,128)(2,1)S(1)} %collective-permute-done.7), channel_id=1, source_target_pairs={{0,2},{1,5},{2,0},{3,7},{4,6},{5,1},{6,4},{7,3},{8,10},{9,13},{10,... | collective-permute-start | bytes 884744 | tf_op jit(solution)/shard_map/ppermute | solution.py:268
  52.6 0.1 collective-permute-start.4
  52.7 1.9 %collective-permute-start.12 = (bf16[48,3072]{1,0:T(8,128)(2,1)S(1)}, bf16[48,3072]{1,0:T(8,128)(2,1)S(1)}, u32[]{:S(2)}, u32[]{:S(2)}) collective-permute-start(bf16[48,3072]{1,0:T(8,128)(2,1)S(1)} %collective-permute-done.11), channel_id=1, source_target_pairs={{0,2},{1,5},{2,0},{3,7},{4,6},{5,1},{6,4},{7,3},{8,10},{9,13},{10,... | collective-permute-start | bytes 884744 | tf_op jit(solution)/shard_map/ppermute | solution.py:268
  54.6 7.1 %collective-permute-done.2 = bf16[48,3072]{1,0:T(8,128)(2,1)S(1)} collective-permute-done((bf16[48,3072]{1,0:T(8,128)(2,1)S(1)}, bf16[48,3072]{1,0:T(8,128)(2,1)S(1)}, u32[]{:S(2)}, u32[]{:S(2)}) %collective-permute-start.2) | collective-permute-done | bytes 294944 | tf_op jit(solution)/shard_map/ppermute | solution.py:268
  61.7 0.9 collective-permute-start.5
  62.5 5.5 %collective-permute-done.9 = bf16[48,3072]{1,0:T(8,128)(2,1)S(1)} collective-permute-done((bf16[48,3072]{1,0:T(8,128)(2,1)S(1)}, bf16[48,3072]{1,0:T(8,128)(2,1)S(1)}, u32[]{:S(2)}, u32[]{:S(2)}) %collective-permute-start.9) | collective-permute-done | bytes 294944 | tf_op jit(solution)/shard_map/ppermute | solution.py:268
  68.0 0.9 collective-permute-start.13
  68.9 1.2 %collective-permute-start.10 = (bf16[48,3072]{1,0:T(8,128)(2,1)S(1)}, bf16[48,3072]{1,0:T(8,128)(2,1)}, u32[]{:S(2)}, u32[]{:S(2)}) collective-permute-start(bf16[48,3072]{1,0:T(8,128)(2,1)S(1)} %collective-permute-done.8), channel_id=1, source_target_pairs={{0,4},{1,3},{2,6},{3,1},{4,0},{5,7},{6,2},{7,5},{8,12},{9,11},{10,... | collective-permute-start | bytes 884744 | tf_op jit(solution)/shard_map/ppermute | solution.py:268
  70.0 0.9 collective-permute-start.6
  70.9 4.1 %collective-permute-done.12 = bf16[48,3072]{1,0:T(8,128)(2,1)S(1)} collective-permute-done((bf16[48,3072]{1,0:T(8,128)(2,1)S(1)}, bf16[48,3072]{1,0:T(8,128)(2,1)S(1)}, u32[]{:S(2)}, u32[]{:S(2)}) %collective-permute-start.12) | collective-permute-done | bytes 294944 | tf_op jit(solution)/shard_map/ppermute | solution.py:268
  75.0 1.7 %collective-permute-start.14 = (bf16[48,3072]{1,0:T(8,128)(2,1)S(1)}, bf16[48,3072]{1,0:T(8,128)(2,1)}, u32[]{:S(2)}, u32[]{:S(2)}) collective-permute-start(bf16[48,3072]{1,0:T(8,128)(2,1)S(1)} %collective-permute-done.12), channel_id=1, source_target_pairs={{0,4},{1,3},{2,6},{3,1},{4,0},{5,7},{6,2},{7,5},{8,12},{9,11},{10,... | collective-permute-start | bytes 884744 | tf_op jit(solution)/shard_map/ppermute | solution.py:268
  76.7 0.6 compare_select_fusion.3.order_ref
  77.3 2.4 %collective-permute-done.10 = bf16[48,3072]{1,0:T(8,128)(2,1)} collective-permute-done((bf16[48,3072]{1,0:T(8,128)(2,1)S(1)}, bf16[48,3072]{1,0:T(8,128)(2,1)}, u32[]{:S(2)}, u32[]{:S(2)}) %collective-permute-start.10) | collective-permute-done | bytes 294944 | tf_op jit(solution)/shard_map/ppermute | solution.py:268
  79.7 3.2 %collective-permute-done.6 = bf16[48,3072]{1,0:T(8,128)(2,1)} collective-permute-done((bf16[48,3072]{1,0:T(8,128)(2,1)S(1)}, bf16[48,3072]{1,0:T(8,128)(2,1)}, u32[]{:S(2)}, u32[]{:S(2)}) %collective-permute-start.6) | collective-permute-done | bytes 294944 | tf_op jit(solution)/shard_map/ppermute | solution.py:268
  82.9 3.2 %collective-permute-done.14 = bf16[48,3072]{1,0:T(8,128)(2,1)} collective-permute-done((bf16[48,3072]{1,0:T(8,128)(2,1)S(1)}, bf16[48,3072]{1,0:T(8,128)(2,1)}, u32[]{:S(2)}, u32[]{:S(2)}) %collective-permute-start.14) | collective-permute-done | bytes 294944 | tf_op jit(solution)/shard_map/ppermute | solution.py:268
  86.1 0.7 copy-done.2
  86.8 5.3 %mix.1 = (bf16[128,3072]{1,0:T(8,128)(2,1)}, f32[128,3072]{1,0:T(8,128)}) custom-call(s32[17]{0:T(128)} %compare_select_fusion.3.order_ref, bf16[16,48,256]{2,1,0:T(8,128)(2,1)} %copy-done.2, bf16[1,48,3072]{2,1,0:T(8,128)(2,1)} %bitcast.109, bf16[1,48,3072]{2,1,0:T(8,128)(2,1)} %bitcast.111, bf16[1,48,3072]{2,1,0:T(8,128)(2,1)} %bitcast.110, ...), custom_call_target="tpu_custom_call" | custom-call | flops 1207959552 | bytes 4718592 | tf_op jit(solution)/shard_map/mix/pallas_call | solution.py:322
  92.1 2.5 %collective-permute-done.15.arrived_ref = bf16[128,3072]{1,0:T(8,128)(2,1)S(1)} collective-permute-done((bf16[128,3072]{1,0:T(8,128)(2,1)}, bf16[128,3072]{1,0:T(8,128)(2,1)S(1)}, u32[]{:S(2)}, u32[]{:S(2)}) %collective-permute-start.15) | collective-permute-done | bytes 786464 | tf_op jit(solution)/shard_map/ppermute | solution.py:390
  94.6 0.9 copy-done.3
  95.4 2.5 %finish.1 = bf16[128,1536]{1,0:T(8,128)(2,1)} custom-call(f32[128,3072]{1,0:T(8,128)} %get-tuple-element.7.ours_ref, bf16[128,3072]{1,0:T(8,128)(2,1)} %copy-done.3), custom_call_target="tpu_custom_call" | custom-call | flops 1572864 | bytes 2752512 | tf_op jit(solution)/shard_map/finish/pallas_call | solution.py:352
  (49 shorter events, 0.2 us)
Async XLA Ops:
  0.0 24.6 %copy-start = (f32[1536]{0:T(1024)S(1)}, f32[1536]{0:T(1024)}, u32[]{:S(2)}) copy-start(f32[1536]{0:T(1024)} %param.19) | copy-start | bytes 18436
  0.0 14.3 %copy-start.15 = (f32[2,64]{1,0:T(2,128)S(1)}, f32[2,64]{1,0:T(2,128)}, u32[]{:S(2)}) copy-start(f32[2,64]{1,0:T(2,128)} %param.16) | copy-start | bytes 1540
  0.0 16.0 %copy-start.16 = (f32[2,64]{1,0:T(2,128)S(1)}, f32[2,64]{1,0:T(2,128)}, u32[]{:S(2)}) copy-start(f32[2,64]{1,0:T(2,128)} %param.15) | copy-start | bytes 1540
  0.0 52.5 %collective-permute-start.1 = (bf16[48,3072]{1,0:T(8,128)(2,1)}, bf16[48,3072]{1,0:T(8,128)(2,1)S(1)}, u32[]{:S(2)}, u32[]{:S(2)}) collective-permute-start(bf16[48,3072]{1,0:T(8,128)(2,1)} %param.20), channel_id=1, source_target_pairs={{0,4},{1,3},{2,6},{3,1},{4,0},{5,7},{6,2},{7,5},{8,12},{9,11},{10,... | collective-permute-start | bytes 884744 | tf_op jit(solution)/shard_map/ppermute | solution.py:268
  3.1 45.4 %collective-permute-start = (bf16[48,3072]{1,0:T(8,128)(2,1)}, bf16[48,3072]{1,0:T(8,128)(2,1)S(1)}, u32[]{:S(2)}, u32[]{:S(2)}) collective-permute-start(bf16[48,3072]{1,0:T(8,128)(2,1)} %param.20), channel_id=1, source_target_pairs={{0,2},{1,5},{2,0},{3,7},{4,6},{5,1},{6,4},{7,3},{8,10},{9,13},{10,... | collective-permute-start | bytes 884744 | tf_op jit(solution)/shard_map/ppermute | solution.py:268
  4.6 46.0 %collective-permute-start.7 = (bf16[48,3072]{1,0:T(8,128)(2,1)}, bf16[48,3072]{1,0:T(8,128)(2,1)S(1)}, u32[]{:S(2)}, u32[]{:S(2)}) collective-permute-start(bf16[48,3072]{1,0:T(8,128)(2,1)} %param.20), channel_id=1, source_target_pairs={{0,24},{1,25},{2,26},{3,27},{4,28},{5,29},{6,30},{7,31},{8,0},{9,1... | collective-permute-start | bytes 884744 | tf_op jit(solution)/shard_map/ppermute | solution.py:268
  8.2 14.8 %collective-permute-start.3 = (bf16[48,3072]{1,0:T(8,128)(2,1)}, bf16[48,3072]{1,0:T(8,128)(2,1)S(1)}, u32[]{:S(2)}, u32[]{:S(2)}) collective-permute-start(bf16[48,3072]{1,0:T(8,128)(2,1)} %param.20), channel_id=1, source_target_pairs={{0,8},{1,9},{2,10},{3,11},{4,12},{5,13},{6,14},{7,15},{8,16},{9,17... | collective-permute-start | bytes 884744 | tf_op jit(solution)/shard_map/ppermute | solution.py:268
  10.1 27.2 %all-to-all-start = ((bf16[32,48,128]{2,1,0:T(8,128)(2,1)}), bf16[32,48,128]{2,1,0:T(8,128)(2,1)S(1)}, u32[]{:S(2)}, u32[]{:S(2)}) async-start(bf16[32,48,128]{2,1,0:T(8,128)(2,1)} %bitcast.1), calls=%async_computation | async-start | bytes 786432 | tf_op jit(solution)/shard_map/all_to_all | solution.py:372
  16.2 9.8 %copy-start.14 = (f32[288,128]{1,0:T(8,128)}, f32[288,128]{1,0:T(8,128)S(1)}, u32[]{:S(2)}) copy-start(f32[288,128]{1,0:T(8,128)S(1)} %fusion.5.left_ref) | copy-start | bytes 442372
  23.0 38.6 %copy-start.7 = (bf16[48,3072]{1,0:T(8,128)(2,1)}, bf16[48,3072]{1,0:T(8,128)(2,1)S(1)}, u32[]{:S(2)}) copy-start(bf16[48,3072]{1,0:T(8,128)(2,1)S(1)} %collective-permute-done.3) | copy-start | bytes 884740
  23.0 29.6 %collective-permute-start.11 = (bf16[48,3072]{1,0:T(8,128)(2,1)S(1)}, bf16[48,3072]{1,0:T(8,128)(2,1)S(1)}, u32[]{:S(2)}, u32[]{:S(2)}) collective-permute-start(bf16[48,3072]{1,0:T(8,128)(2,1)S(1)} %collective-permute-done.3), channel_id=1, source_target_pairs={{0,8},{1,9},{2,10},{3,11},{4,12},{5,13},{6,14},{7,15},{8,16},{9,17... | collective-permute-start | bytes 884744 | tf_op jit(solution)/shard_map/ppermute | solution.py:268
  37.3 0.7 copy-start.1
  44.4 41.6 %all-to-all-start.1 = ((bf16[16,48,256]{2,1,0:T(8,128)(2,1)}), bf16[16,48,256]{2,1,0:T(8,128)(2,1)S(1)}, u32[]{:S(2)}, u32[]{:S(2)}) async-start(bf16[16,48,256]{2,1,0:T(8,128)(2,1)} %conv.1), calls=%async_computation.1 | async-start | bytes 786432 | tf_op jit(solution)/shard_map/all_to_all | solution.py:388
  48.5 37.5 %copy-start.5 = (bf16[48,3072]{1,0:T(8,128)(2,1)}, bf16[48,3072]{1,0:T(8,128)(2,1)S(1)}, u32[]{:S(2)}) copy-start(bf16[48,3072]{1,0:T(8,128)(2,1)S(1)} %collective-permute-done) | copy-start | bytes 884740
  48.5 13.1 %collective-permute-start.2 = (bf16[48,3072]{1,0:T(8,128)(2,1)S(1)}, bf16[48,3072]{1,0:T(8,128)(2,1)S(1)}, u32[]{:S(2)}, u32[]{:S(2)}) collective-permute-start(bf16[48,3072]{1,0:T(8,128)(2,1)S(1)} %collective-permute-done), channel_id=1, source_target_pairs={{0,4},{1,3},{2,6},{3,1},{4,0},{5,7},{6,2},{7,5},{8,12},{9,11},{10,... | collective-permute-start | bytes 884744 | tf_op jit(solution)/shard_map/ppermute | solution.py:268
  50.5 35.5 %copy-start.6 = (bf16[48,3072]{1,0:T(8,128)(2,1)}, bf16[48,3072]{1,0:T(8,128)(2,1)S(1)}, u32[]{:S(2)}) copy-start(bf16[48,3072]{1,0:T(8,128)(2,1)S(1)} %collective-permute-done.7) | copy-start | bytes 884740
  50.5 17.5 %collective-permute-start.9 = (bf16[48,3072]{1,0:T(8,128)(2,1)S(1)}, bf16[48,3072]{1,0:T(8,128)(2,1)S(1)}, u32[]{:S(2)}, u32[]{:S(2)}) collective-permute-start(bf16[48,3072]{1,0:T(8,128)(2,1)S(1)} %collective-permute-done.7), channel_id=1, source_target_pairs={{0,4},{1,3},{2,6},{3,1},{4,0},{5,7},{6,2},{7,5},{8,12},{9,11},{10,... | collective-permute-start | bytes 884744 | tf_op jit(solution)/shard_map/ppermute | solution.py:268
  50.6 18.2 %collective-permute-start.8 = (bf16[48,3072]{1,0:T(8,128)(2,1)S(1)}, bf16[48,3072]{1,0:T(8,128)(2,1)S(1)}, u32[]{:S(2)}, u32[]{:S(2)}) collective-permute-start(bf16[48,3072]{1,0:T(8,128)(2,1)S(1)} %collective-permute-done.7), channel_id=1, source_target_pairs={{0,2},{1,5},{2,0},{3,7},{4,6},{5,1},{6,4},{7,3},{8,10},{9,13},{10,... | collective-permute-start | bytes 884744 | tf_op jit(solution)/shard_map/ppermute | solution.py:268
  52.6 33.5 %copy-start.4 = (bf16[48,3072]{1,0:T(8,128)(2,1)}, bf16[48,3072]{1,0:T(8,128)(2,1)S(1)}, u32[]{:S(2)}) copy-start(bf16[48,3072]{1,0:T(8,128)(2,1)S(1)} %collective-permute-done.1) | copy-start | bytes 884740
  52.6 17.5 %collective-permute-start.4 = (bf16[48,3072]{1,0:T(8,128)(2,1)S(1)}, bf16[48,3072]{1,0:T(8,128)(2,1)S(1)}, u32[]{:S(2)}, u32[]{:S(2)}) collective-permute-start(bf16[48,3072]{1,0:T(8,128)(2,1)S(1)} %collective-permute-done.3), channel_id=1, source_target_pairs={{0,2},{1,5},{2,0},{3,7},{4,6},{5,1},{6,4},{7,3},{8,10},{9,13},{10,... | collective-permute-start | bytes 884744 | tf_op jit(solution)/shard_map/ppermute | solution.py:268
  52.7 33.4 %copy-start.8 = (bf16[48,3072]{1,0:T(8,128)(2,1)}, bf16[48,3072]{1,0:T(8,128)(2,1)S(1)}, u32[]{:S(2)}) copy-start(bf16[48,3072]{1,0:T(8,128)(2,1)S(1)} %collective-permute-done.11) | copy-start | bytes 884740
  52.7 22.3 %collective-permute-start.12 = (bf16[48,3072]{1,0:T(8,128)(2,1)S(1)}, bf16[48,3072]{1,0:T(8,128)(2,1)S(1)}, u32[]{:S(2)}, u32[]{:S(2)}) collective-permute-start(bf16[48,3072]{1,0:T(8,128)(2,1)S(1)} %collective-permute-done.11), channel_id=1, source_target_pairs={{0,2},{1,5},{2,0},{3,7},{4,6},{5,1},{6,4},{7,3},{8,10},{9,13},{10,... | collective-permute-start | bytes 884744 | tf_op jit(solution)/shard_map/ppermute | solution.py:268
  61.7 24.4 %copy-start.9 = (bf16[48,3072]{1,0:T(8,128)(2,1)}, bf16[48,3072]{1,0:T(8,128)(2,1)S(1)}, u32[]{:S(2)}) copy-start(bf16[48,3072]{1,0:T(8,128)(2,1)S(1)} %collective-permute-done.2) | copy-start | bytes 884740
  61.7 15.6 %collective-permute-start.5 = (bf16[48,3072]{1,0:T(8,128)(2,1)S(1)}, bf16[48,3072]{1,0:T(8,128)(2,1)}, u32[]{:S(2)}, u32[]{:S(2)}) collective-permute-start(bf16[48,3072]{1,0:T(8,128)(2,1)S(1)} %collective-permute-done.3), channel_id=1, source_target_pairs={{0,4},{1,3},{2,6},{3,1},{4,0},{5,7},{6,2},{7,5},{8,12},{9,11},{10,... | collective-permute-start | bytes 884744 | tf_op jit(solution)/shard_map/ppermute | solution.py:268
  68.0 18.1 %copy-start.10 = (bf16[48,3072]{1,0:T(8,128)(2,1)}, bf16[48,3072]{1,0:T(8,128)(2,1)S(1)}, u32[]{:S(2)}) copy-start(bf16[48,3072]{1,0:T(8,128)(2,1)S(1)} %collective-permute-done.9) | copy-start | bytes 884740
  68.0 11.7 %collective-permute-start.13 = (bf16[48,3072]{1,0:T(8,128)(2,1)S(1)}, bf16[48,3072]{1,0:T(8,128)(2,1)}, u32[]{:S(2)}, u32[]{:S(2)}) collective-permute-start(bf16[48,3072]{1,0:T(8,128)(2,1)S(1)} %collective-permute-done.11), channel_id=1, source_target_pairs={{0,4},{1,3},{2,6},{3,1},{4,0},{5,7},{6,2},{7,5},{8,12},{9,11},{10,... | collective-permute-start | bytes 884744 | tf_op jit(solution)/shard_map/ppermute | solution.py:268
  68.8 17.2 %copy-start.11 = (bf16[48,3072]{1,0:T(8,128)(2,1)}, bf16[48,3072]{1,0:T(8,128)(2,1)S(1)}, u32[]{:S(2)}) copy-start(bf16[48,3072]{1,0:T(8,128)(2,1)S(1)} %collective-permute-done.8) | copy-start | bytes 884740
  68.9 10.8 %collective-permute-start.10 = (bf16[48,3072]{1,0:T(8,128)(2,1)S(1)}, bf16[48,3072]{1,0:T(8,128)(2,1)}, u32[]{:S(2)}, u32[]{:S(2)}) collective-permute-start(bf16[48,3072]{1,0:T(8,128)(2,1)S(1)} %collective-permute-done.8), channel_id=1, source_target_pairs={{0,4},{1,3},{2,6},{3,1},{4,0},{5,7},{6,2},{7,5},{8,12},{9,11},{10,... | collective-permute-start | bytes 884744 | tf_op jit(solution)/shard_map/ppermute | solution.py:268
  70.0 16.1 %copy-start.12 = (bf16[48,3072]{1,0:T(8,128)(2,1)}, bf16[48,3072]{1,0:T(8,128)(2,1)S(1)}, u32[]{:S(2)}) copy-start(bf16[48,3072]{1,0:T(8,128)(2,1)S(1)} %collective-permute-done.4) | copy-start | bytes 884740
  70.0 12.8 %collective-permute-start.6 = (bf16[48,3072]{1,0:T(8,128)(2,1)S(1)}, bf16[48,3072]{1,0:T(8,128)(2,1)}, u32[]{:S(2)}, u32[]{:S(2)}) collective-permute-start(bf16[48,3072]{1,0:T(8,128)(2,1)S(1)} %collective-permute-done.4), channel_id=1, source_target_pairs={{0,4},{1,3},{2,6},{3,1},{4,0},{5,7},{6,2},{7,5},{8,12},{9,11},{10,... | collective-permute-start | bytes 884744 | tf_op jit(solution)/shard_map/ppermute | solution.py:268
  75.0 11.1 %copy-start.13 = (bf16[48,3072]{1,0:T(8,128)(2,1)}, bf16[48,3072]{1,0:T(8,128)(2,1)S(1)}, u32[]{:S(2)}) copy-start(bf16[48,3072]{1,0:T(8,128)(2,1)S(1)} %collective-permute-done.12) | copy-start | bytes 884740
  75.0 11.1 %collective-permute-start.14 = (bf16[48,3072]{1,0:T(8,128)(2,1)S(1)}, bf16[48,3072]{1,0:T(8,128)(2,1)}, u32[]{:S(2)}, u32[]{:S(2)}) collective-permute-start(bf16[48,3072]{1,0:T(8,128)(2,1)S(1)} %collective-permute-done.12), channel_id=1, source_target_pairs={{0,4},{1,3},{2,6},{3,1},{4,0},{5,7},{6,2},{7,5},{8,12},{9,11},{10,... | collective-permute-start | bytes 884744 | tf_op jit(solution)/shard_map/ppermute | solution.py:268
  86.0 0.7 copy-start.2
  92.1 2.5 %collective-permute-start.15 = (bf16[128,3072]{1,0:T(8,128)(2,1)}, bf16[128,3072]{1,0:T(8,128)(2,1)S(1)}, u32[]{:S(2)}, u32[]{:S(2)}) collective-permute-start(bf16[128,3072]{1,0:T(8,128)(2,1)} %get-tuple-element.8), channel_id=1, source_target_pairs={{0,1},{1,0},{2,3},{3,2},{4,5},{5,4},{6,7},{7,6},{8,9},{9,8},{10,11... | collective-permute-start | bytes 2359304 | tf_op jit(solution)/shard_map/ppermute | solution.py:390
  94.5 0.9 copy-start.3

commit v3 on v2

--- a/solution.py
+++ b/solution.py
@@ -59,12 +59,22 @@
     cosine, sine = np.cos(inner), np.sin(inner)
     forward = np.block([[cosine, -sine], [sine, cosine]])
     inverse = np.block([[cosine, sine], [-sine, cosine]])
+    turns = np.concatenate(split_table(twiddle.reshape(2 * rows, tok_rows)), 1)
+    parts, places, at = [], [], 0
+    for table in (first, turns, last, forward, inverse):
+        height = -(-table.shape[0] // 16) * 16
+        filled = np.zeros((height, 2 * tok_rows))
+        filled[: table.shape[0], : table.shape[1]] = table
+        parts.append(filled)
+        places.append((at, *table.shape))
+        at += height
+    return jnp.asarray(np.concatenate(parts, 0), BF16), tuple(places)
+
+
+def complex_mul(first, second):
     return (
-        jnp.asarray(first, BF16),
-        jnp.asarray(twiddle, F32),
-        jnp.asarray(forward, BF16),
-        jnp.asarray(inverse, BF16),
-        jnp.asarray(last, BF16),
+        first[0] * second[0] - first[1] * second[1],
+        first[0] * second[1] + first[1] * second[0],
     )
 
 
@@ -76,15 +86,46 @@
     return high, middle, low
 
 
-def response_kernel(chans, group, width, tab_ref, rates_ref, left_ref, out_ref):
+def column_of(row):
+    size = row.shape[1]
+    if size < 128:
+        row = jnp.concatenate([row, jnp.zeros((1, 128 - size), row.dtype)], 1)
+    return jnp.broadcast_to(row, (8, 128)).T[:size, 0:1]
+
+
+def response_kernel(
+    group, width, tab_ref, rates_ref, low_ref, in_ref, out_proj_ref, out_ref, left_a, left_b, side
+):
+    _, chans = in_ref.shape[1:]
+    total = 6 * chans
+
+    @pl.when(pl.program_id(0) == 0)
+    def _():
+        low = (low_ref[0:1, :], low_ref[1:2, :])
+        low_conj = (low[0], -low[1])
+        side[:, 0:1] = column_of(-rates_ref[0:1, :])
+        side[:, 1:2] = column_of(rates_ref[1:2, :])
+        side[:, 2:3] = column_of(low[0] * low[0] + low[1] * low[1])
+        in_pair = (in_ref[0].T, in_ref[1].T)
+        out_pair = (out_proj_ref[0].T, out_proj_ref[1].T)
+        blocks = []
+        for first, second in ((out_pair, in_pair), (out_pair, low), (low_conj, in_pair)):
+            real, imag = complex_mul(first, second)
+            blocks.append(jnp.concatenate([real, -imag], 1))
+            blocks.append(jnp.concatenate([imag, real], 1))
+        high, middle, low_part = thirds(jnp.concatenate(blocks, 0))
+        left_a[:total, :] = jnp.concatenate([middle, middle], 1)
+        left_a[total:, :] = jnp.concatenate([high, high], 1)
+        left_b[...] = jnp.concatenate([high, low_part], 1)
+
     cos_half = tab_ref[0, 0:1, :]
     sin_half = tab_ref[0, 1:2, :]
     weight = tab_ref[0, 2:3, :]
     cos_two = jnp.concatenate([cos_half, cos_half], 1)
     sin_two = jnp.concatenate([sin_half, -sin_half], 1)
-    decay = -rates_ref[:, 0:1]
-    spin = rates_ref[:, 1:2]
-    power = rates_ref[:, 2:3]
+    decay = side[:, 0:1]
+    spin = side[:, 1:2]
+    power = side[:, 2:3]
     real_part = cos_two * decay
     imag_part = -(2.0 * sin_two + cos_two * spin)
     inv_norm = 1.0 / (real_part * real_part + imag_part * imag_part)
@@ -98,17 +139,10 @@
     d_real = den_real * den_inv
     d_imag = -den_imag * den_inv
     v_high, v_mid, v_low = thirds(jnp.concatenate([v_real, v_imag], 0))
-    l_high, l_mid, l_low = thirds(left_ref[...])
     right_a = jnp.concatenate([v_high, v_mid], 0)
     right_b = jnp.concatenate([v_low, v_high], 0)
-
-    left_b = jnp.concatenate([l_high, l_low], 1)
-    left_a = jnp.concatenate(
-        [jnp.concatenate([l_mid, l_mid], 1), jnp.concatenate([l_high, l_high], 1)], 0
-    )
-    part_a = jnp.dot(left_a, right_a, preferred_element_type=F32)
-    part_b = jnp.dot(left_b, right_b, preferred_element_type=F32)
-    total = 6 * chans
+    part_a = jnp.dot(left_a[...], right_a, preferred_element_type=F32)
+    part_b = jnp.dot(left_b[...], right_b, preferred_element_type=F32)
     sums = (part_b + part_a[:total]) + part_a[total:]
     cb_real, cb_imag, cp_real, cp_imag, pb_real, pb_imag = [
         sums[i * chans : (i + 1) * chans] for i in range(6)
@@ -128,45 +162,55 @@
         out_ref[g, :, width:] = s_imag[:, cols]
 
 
-def half_spectrum(tables, rates, left, chans, width, group):
-    pairs = tables.shape[1]
-    steps = pairs // group
-    states = rates.shape[0]
-    tables = tables.reshape(3, steps, group * width).transpose(1, 0, 2)
-    tables = jnp.asarray(tables)
+def half_spectrum(tables, start, steps, rates, low, in_own, out_own, width, group):
+    pairs = steps * group
+    states, chans = in_own.shape[1:]
+    whole = lambda value: pl.BlockSpec(value.shape, lambda i: (0,) * value.ndim)
     return pl.pallas_call(
-        functools.partial(response_kernel, chans, group, width),
+        functools.partial(response_kernel, group, width),
         grid=(steps,),
         in_specs=[
-            pl.BlockSpec((1, 3, group * width), lambda i: (i, 0, 0)),
-            pl.BlockSpec((states, 3), lambda i: (0, 0)),
-            pl.BlockSpec((6 * chans, 2 * states), lambda i: (0, 0)),
+            pl.BlockSpec((1, 3, group * width), lambda i: (i + start, 0, 0)),
+            whole(rates),
+            whole(low),
+            whole(in_own),
+            whole(out_own),
         ],
         out_specs=pl.BlockSpec((group, chans, 2 * width), lambda i: (i, 0, 0)),
         out_shape=jax.ShapeDtypeStruct((pairs, chans, 2 * width), F32),
+        scratch_shapes=[
+            pltpu.VMEM((12 * chans, 4 * states), BF16),
+            pltpu.VMEM((6 * chans, 4 * states), BF16),
+            pltpu.VMEM((states, 128), F32),
+        ],
         cost_estimate=pl.CostEstimate(
             flops=pairs * width * chans * states * 48, bytes_accessed=1 << 21, transcendentals=0
         ),
+        compiler_params=pltpu.CompilerParams(vmem_limit_bytes=12 << 20),
         name="response",
-    )(tables, rates, left)
-
-
-def conv_kernel(
-    seq_count, chans, width,
-    x_ref, s_ref, t_ref, skip_ref, first_ref, tw_ref, forward_ref, inverse_ref, last_ref,
-    out_ref, xf, ar, ai,
-):
+    )(tables, rates, low, in_own, out_own)
+
+
+def conv_kernel(seq_count, chans, width, places, x_ref, *refs):
+    s_refs, (skip_ref, tab_ref, out_ref, xf, ar, ai) = refs[:PARTS], refs[PARTS:]
     pairs = seq_count + 1
     rows = padded(pairs)
     bundle = 4
     for s in range(seq_count):
         xf[s * chans : (s + 1) * chans, :] = x_ref[s].astype(F32)
-    tw_cos, tw_sin = tw_ref[0], tw_ref[1]
+    first, turns, last, forward, inverse = [
+        (lambda at=at, height=height, wide=wide: tab_ref[at : at + height, :wide])
+        for at, height, wide in places
+    ]
+    turn = turns().astype(F32)
+    turn = turn[:, :width] + turn[:, width:]
+    tw_cos, tw_sin = turn[:rows], turn[rows:]
+    skip_col = column_of(skip_ref[...])
     for base in range(0, chans, bundle):
         parts = [xf[pl.ds(base + j, seq_count, stride=chans), :] for j in range(bundle)]
         right = jnp.concatenate(parts, 1).astype(BF16)
         right = jnp.concatenate([right, right], 0)
-        got = jnp.dot(first_ref[...], right, preferred_element_type=F32)
+        got = jnp.dot(first(), right, preferred_element_type=F32)
         for j in range(bundle):
             cols = slice(j * width, (j + 1) * width)
             real, imag = got[:rows, cols], got[rows:, cols]
@@ -179,20 +223,22 @@
         def step(index, carry):
             at = pl.ds(pl.multiple_of(start * chans + index * span, 8), span)
             left = jnp.concatenate([ar[at, :], ai[at, :]], 1).astype(BF16)
-            spec = jnp.dot(left, forward_ref[...], preferred_element_type=F32)
+            spec = jnp.dot(left, forward(), preferred_element_type=F32)
             filt = source[pl.ds(index * per_loop, per_loop)].reshape(span, 2 * width)
             x_r, x_i = spec[:, :width], spec[:, width:]
             f_r, f_i = filt[:, :width], filt[:, width:]
             prod = jnp.concatenate([x_r * f_r - x_i * f_i, x_r * f_i + x_i * f_r], 1)
-            back = jnp.dot(prod.astype(BF16), inverse_ref[...], preferred_element_type=F32)
+            back = jnp.dot(prod.astype(BF16), inverse(), preferred_element_type=F32)
             ar[at, :] = back[:, :width]
             ai[at, :] = back[:, width:]
             return carry
 
         lax.fori_loop(0, source.shape[0] // per_loop, step, 0)
 
-    filter_rows(s_ref, 0, group_of(s_ref.shape[0], 13))
-    filter_rows(t_ref, s_ref.shape[0], group_of(t_ref.shape[0], 13))
+    start = 0
+    for source in s_refs:
+        filter_rows(source, start, group_of(source.shape[0], 13))
+        start += source.shape[0]
 
     for base in range(0, chans, bundle):
         parts = []
@@ -205,10 +251,10 @@
                 )
             )
         right = jnp.concatenate(parts, 1).astype(BF16)
-        got = jnp.dot(last_ref[...], right, preferred_element_type=F32)
+        got = jnp.dot(last(), right, preferred_element_type=F32)
         for j in range(bundle):
             at = pl.ds(base + j, seq_count, stride=chans)
-            skip = skip_ref[base + j : base + j + 1, :]
+            skip = skip_col[base + j : base + j + 1, :]
             xf[at, :] = got[:, j * width : (j + 1) * width] + skip * xf[at, :]
     for s in range(seq_count):
         pre = xf[s * chans : (s + 1) * chans, :]
@@ -218,9 +264,11 @@
 
 def filtered(columns, spectrum, skip, seq_count, chans, width):
     pairs = seq_count + 1
-    tables = conv_tables(seq_count, width)
+    tables, places = conv_tables(seq_count, width)
     return pl.pallas_call(
-        functools.partial(conv_kernel, seq_count, chans, width),
+        functools.partial(conv_kernel, seq_count, chans, width, places),
+        in_specs=[pl.BlockSpec(memory_space=pltpu.VMEM)] * (3 + PARTS),
+        out_specs=pl.BlockSpec(memory_space=pltpu.VMEM),
         out_shape=jax.ShapeDtypeStruct((seq_count // 2, chans, 2 * width), BF16),
         scratch_shapes=[
             pltpu.VMEM((seq_count * chans, width), F32),
@@ -230,29 +278,13 @@
         cost_estimate=pl.CostEstimate(
             flops=1 << 29, bytes_accessed=1 << 21, transcendentals=1 << 18
         ),
+        compiler_params=pltpu.CompilerParams(vmem_limit_bytes=14 << 20),
         name="conv",
-    )(columns, *spectrum, skip, *tables)
-
-
-def complex_mul(first, second):
-    return (
-        first[0] * second[0] - first[1] * second[1],
-        first[0] * second[1] + first[1] * second[0],
-    )
-
-
-def left_matrix(coupling, in_own, out_own):
-    low = (coupling[0][:, None], coupling[1][:, None])
-    low_conj = (low[0], -low[1])
-    blocks = []
-    for first, second in ((out_own, in_own), (out_own, low), (low_conj, in_own)):
-        real, imag = complex_mul(first, second)
-        blocks.append(jnp.concatenate([real, -imag], 0).T)
-        blocks.append(jnp.concatenate([imag, real], 0).T)
-    return jnp.concatenate(blocks, 0)
+    )(columns, *spectrum, skip, tables)
 
 
 AXES = ("chip", "core")
+PARTS = 1
 
 
 def weight_pieces(mix_weight, chip_count):
@@ -334,6 +366,7 @@
             bytes_accessed=chips * chans * cols * 2,
             transcendentals=0,
         ),
+        compiler_params=pltpu.CompilerParams(vmem_limit_bytes=24 << 20),
         name="mix",
     )(table.astype(jnp.int32), act, *pieces)
 
@@ -344,7 +377,7 @@
         at, gate_at = slice(col, col + 256), slice(cols + col, cols + col + 256)
         value = ours_ref[:, at] + arrived_ref[:, at].astype(F32)
         gate = ours_ref[:, gate_at] + arrived_ref[:, gate_at].astype(F32)
-        out_ref[:, at] = (value * jax.nn.sigmoid(gate)).astype(BF16)
+        out_ref[:, at] = (value * (0.5 + 0.5 * jnp.tanh(0.5 * gate))).astype(BF16)
 
 
 def finished(ours, arrived):
@@ -357,6 +390,7 @@
         cost_estimate=pl.CostEstimate(
             flops=rows * cols * 4, bytes_accessed=rows * cols * 7, transcendentals=rows * cols
         ),
+        compiler_params=pltpu.CompilerParams(vmem_limit_bytes=8 << 20),
         name="finish",
     )(ours, arrived)
 
@@ -371,19 +405,25 @@
     columns = tokens.T.reshape(seq_count, chans, width)
     columns = lax.all_to_all(columns, AXES, 0, 0)
     pieces, order = weight_pieces(mix_weight, chip_count)
-    skip = lax.dynamic_slice_in_dim(skip_gain, place * chans, chans, 0)[:, None]
+    skip = lax.dynamic_slice_in_dim(skip_gain, place * chans, chans, 0)[None]
     in_own = lax.dynamic_slice_in_dim(in_proj, place * chans, chans, 2)
     out_own = lax.dynamic_slice_in_dim(out_proj, place * chans, chans, 2)
-    left = left_matrix(coupling, in_own, out_own)
-    power = coupling[0] * coupling[0] + coupling[1] * coupling[1]
-    rates = jnp.stack([state_rates[0], state_rates[1], power], 1)
+    in_own, out_own, skip = lax.optimization_barrier((in_own, out_own, skip))
     tables = half_angles(seq_count, width)
-    pairs = tables.shape[1]
-    group = group_of(pairs, 6)
-    cut = -(-pairs // group // 2) * group
+    group = group_of(tables.shape[1], 6)
+    steps = tables.shape[1] // group
+    tables = tables.reshape(3, steps, group * width).transpose(1, 0, 2)
+    tables = jnp.asarray(tables)
+    cut = -(-steps // PARTS)
     spectrum = []
-    for part in (tables[:, :cut], tables[:, cut:]):
-        spectrum.append(half_spectrum(part, rates, left, chans, width, group))
+    for index in range(PARTS):
+        start = index * cut
+        count = min(cut, steps - start)
+        spectrum.append(
+            half_spectrum(
+                tables, start, count, state_rates, coupling, in_own, out_own, width, group
+            )
+        )
     activation = filtered(columns, spectrum, skip, seq_count, chans, width)
     act = lax.all_to_all(activation, "chip", 0, 0)
     theirs, ours = mixed(act, pieces, order, core, width)

time: 98.7 us -> 96.5 us (0.978)
  Pallas kernels: 25.4 us -> 16.4 us
  starting transfers between devices: 29.6 us -> 37.1 us
  waiting for transfers between devices: 34.6 us -> 39.4 us
  local copies, waits for them, and re-layouts: 7.08 us -> 3.11 us
  other arithmetic: 1.12 us -> 0.02 us
    pallas_call x3 -> x2, Pallas kernels: 17.6 us -> 12.4 us  [the longest x1 8.27 us: half_spectrum(): pl.pallas_call(functools.partial(response_kernel, group, width), grid=(st...]
    ppermute x15, waiting for transfers between devices: 32.1 us -> 37.1 us  [moved(): return lax.ppermute(value, AXES, pairs)]
    all_to_all x1, starting transfers between devices: 4.19 us -> 7.36 us  [shards(): columns = lax.all_to_all(columns, AXES, 0, 0)]
    ppermute x15, starting transfers between devices: 21.2 us -> 24 us  [moved(): return lax.ppermute(value, AXES, pairs)]
    unnamed x38 -> x12, local copies, waits for them, and re-layouts: 2.64 us -> 0.03 us
    pallas_call x1, Pallas kernels: 5.28 us -> 2.97 us  [mixed(): pl.pallas_call(functools.partial(mix_kernel, width), in_specs=[pl.BlockSp...]
    all_to_all x1, starting transfers between devices: 4.12 us -> 5.68 us  [shards(): act = lax.all_to_all(activation, 'chip', 0, 0)]
    pallas_call x1, Pallas kernels: 2.55 us -> 1.02 us  [finished(): pl.pallas_call(finish_kernel, in_specs=[pl.BlockSpec(memory_space=pltpu.V...]
  transfers between devices with their start and end apart: 18 -> 18, of which waited for: 8 -> 8; matrix products, arithmetic and copies ran while one was open for 6% -> 1% of each run, Pallas kernels for 18% -> 13%
where the time goes in v3:
time: 96.5 us; the launch traced here: 96.1 us
  waiting for transfers between devices  39.4 us (41%)
  starting transfers between devices  37.1 us (38%)
  Pallas kernels  16.4 us (17%)
  local copies, waits for them, and re-layouts  3.11 us (3%)
    ppermute x15, waiting for transfers between devices, moved(): return lax.ppermute(value, AXES, pairs)  37.1 us
    ppermute x15, starting transfers between devices, moved(): return lax.ppermute(value, AXES, pairs)  24 us
    pallas_call x1, Pallas kernels, half_spectrum(): pl.pallas_call(functools.partial(response_kernel, group, width), grid=(st...  8.27 us
    all_to_all x1, starting transfers between devices, shards(): columns = lax.all_to_all(columns, AXES, 0, 0)  7.36 us
    all_to_all x1, starting transfers between devices, shards(): act = lax.all_to_all(activation, 'chip', 0, 0)  5.68 us
    pallas_call x1, Pallas kernels, filtered(): pl.pallas_call(functools.partial(conv_kernel, seq_count, chans, width, pl...  4.16 us
    pallas_call x1, Pallas kernels, mixed(): pl.pallas_call(functools.partial(mix_kernel, width), in_specs=[pl.BlockSp...  2.97 us
    ppermute x1, waiting for transfers between devices, shards(): arrived = lax.ppermute(theirs, 'core', [(0, 1), (1, 0)])  2.27 us
  transfers between devices with their start and end apart: 18, of which 8 were waited for; matrix products, arithmetic and copies ran while one was open for 1% of the time, Pallas kernels for 13%

profile of v3, /device:TPU:0, one launch (start us, length us, event | category | flops | bytes accessed | tf_op | source)
XLA Modules:
  0.0 96.1 jit_solution(11831892394695435904)
XLA Ops:
  0.0 0.0 copy-start
  0.0 1.9 %copy.10 = bf16[1536,128]{1,0:T(8,128)(2,1)} copy(bf16[1536,128]{0,1:T(8,128)(2,1)} %bitcast.29) | data formatting | bytes 786432 | tf_op jit(solution)/shard_map/transpose | solution.py:405
  2.0 7.4 %all-to-all-start = ((bf16[32,48,128]{2,1,0:T(8,128)(2,1)}), bf16[32,48,128]{2,1,0:T(8,128)(2,1)S(1)}, u32[]{:S(2)}, u32[]{:S(2)}) async-start(bf16[32,48,128]{2,1,0:T(8,128)(2,1)} %bitcast.1), calls=%async_computation | async-start | bytes 786432 | tf_op jit(solution)/shard_map/all_to_all | solution.py:406
  9.3 1.8 %collective-permute-start.3 = (bf16[48,3072]{1,0:T(8,128)(2,1)}, bf16[48,3072]{1,0:T(8,128)(2,1)S(1)}, u32[]{:S(2)}, u32[]{:S(2)}) collective-permute-start(bf16[48,3072]{1,0:T(8,128)(2,1)} %param.15), channel_id=1, source_target_pairs={{0,8},{1,9},{2,10},{3,11},{4,12},{5,13},{6,14},{7,15},{8,16},{9,17... | collective-permute-start | bytes 884744 | tf_op jit(solution)/shard_map/ppermute | solution.py:300
  11.2 1.5 %collective-permute-start.1 = (bf16[48,3072]{1,0:T(8,128)(2,1)}, bf16[48,3072]{1,0:T(8,128)(2,1)S(1)}, u32[]{:S(2)}, u32[]{:S(2)}) collective-permute-start(bf16[48,3072]{1,0:T(8,128)(2,1)} %param.15), channel_id=1, source_target_pairs={{0,4},{1,3},{2,6},{3,1},{4,0},{5,7},{6,2},{7,5},{8,12},{9,11},{10,... | collective-permute-start | bytes 884744 | tf_op jit(solution)/shard_map/ppermute | solution.py:300
  12.6 1.5 %collective-permute-start = (bf16[48,3072]{1,0:T(8,128)(2,1)}, bf16[48,3072]{1,0:T(8,128)(2,1)}, u32[]{:S(2)}, u32[]{:S(2)}) collective-permute-start(bf16[48,3072]{1,0:T(8,128)(2,1)} %param.15), channel_id=1, source_target_pairs={{0,2},{1,5},{2,0},{3,7},{4,6},{5,1},{6,4},{7,3},{8,10},{9,13},{10,... | collective-permute-start | bytes 884744 | tf_op jit(solution)/shard_map/ppermute | solution.py:300
  14.1 2.4 %collective-permute-start.7 = (bf16[48,3072]{1,0:T(8,128)(2,1)}, bf16[48,3072]{1,0:T(8,128)(2,1)}, u32[]{:S(2)}, u32[]{:S(2)}) collective-permute-start(bf16[48,3072]{1,0:T(8,128)(2,1)} %param.15), channel_id=1, source_target_pairs={{0,24},{1,25},{2,26},{3,27},{4,28},{5,29},{6,30},{7,31},{8,0},{9,1... | collective-permute-start | bytes 884744 | tf_op jit(solution)/shard_map/ppermute | solution.py:300
  16.4 1.1 %constant_dynamic-slice_fusion = (f32[2,64,48]{2,1,0:T(8,128)S(1)}, f32[2,64,48]{2,1,0:T(8,128)S(1)}) fusion(f32[2,64,1536]{2,1,0:T(8,128)} %param.13, s32[]{:T(128)S(6)} %select_n.62, f32[2,64,1536]{2,1,0:T(8,128)} %param.12), kind=kLoop, calls=%fused_computation.18 | loop fusion | bytes 98308 | tf_op jit(solution)/shard_map/dynamic_slice | solution.py:410
  17.5 9.7 %collective-permute-done.3 = bf16[48,3072]{1,0:T(8,128)(2,1)S(1)} collective-permute-done((bf16[48,3072]{1,0:T(8,128)(2,1)}, bf16[48,3072]{1,0:T(8,128)(2,1)S(1)}, u32[]{:S(2)}, u32[]{:S(2)}) %collective-permute-start.3) | collective-permute-done | bytes 294944 | tf_op jit(solution)/shard_map/ppermute | solution.py:300
  27.2 5.5 %collective-permute-start.11 = (bf16[48,3072]{1,0:T(8,128)(2,1)S(1)}, bf16[48,3072]{1,0:T(8,128)(2,1)}, u32[]{:S(2)}, u32[]{:S(2)}) collective-permute-start(bf16[48,3072]{1,0:T(8,128)(2,1)S(1)} %collective-permute-done.3), channel_id=1, source_target_pairs={{0,8},{1,9},{2,10},{3,11},{4,12},{5,13},{6,14},{7,15},{8,16},{9,17... | collective-permute-start | bytes 884744 | tf_op jit(solution)/shard_map/ppermute | solution.py:300
  32.7 0.0 copy-done
  32.7 0.1 dynamic-slice_bitcast_fusion.refs_1_
  32.8 0.0 copy-done.5
  32.8 0.0 copy-done.4
  32.8 8.3 %response.1.refs_0_ = f32[33,48,256]{2,1,0:T(8,128)S(1)} custom-call(f32[11,3,384]{2,1,0:T(4,128)S(1)} %copy-done.5, f32[2,64]{1,0:T(2,128)S(1)} %copy-done.3, f32[2,64]{1,0:T(2,128)S(1)} %copy-done.4, f32[2,64,48]{2,1,0:T(8,128)S(1)} %get-tuple-element.10.in_ref, f32[2,64,48]{2,1,0:T(8,128)S(1)} %get-tuple-element.11.out_proj_ref), custom_call_target="tpu_custom_call" | custom-call | flops 622854144 | bytes 2097152 | tf_op jit(solution)/shard_map/response/pallas_call | solution.py:169
  41.1 0.0 copy-start.2
  41.1 0.0 all-to-all-done.x_ref
  41.1 4.2 %conv.1 = bf16[16,48,256]{2,1,0:T(8,128)(2,1)} custom-call(bf16[32,48,128]{2,1,0:T(8,128)(2,1)S(1)} %all-to-all-done.x_ref, f32[33,48,256]{2,1,0:T(8,128)S(1)} %response.1.refs_0_, f32[1,48]{1,0:T(1,128)S(1)} %dynamic-slice_bitcast_fusion.refs_1_, bf16[704,256]{1,0:T(8,128)(2,1)S(1)} %copy-done.1), custom_call_target="tpu_custom_call" | custom-call | flops 536870912 | bytes 2097152 | tf_op jit(solution)/shard_map/conv/pallas_call | solution.py:268
  45.3 5.7 %all-to-all-start.1 = ((bf16[16,48,256]{2,1,0:T(8,128)(2,1)}), bf16[16,48,256]{2,1,0:T(8,128)(2,1)S(1)}, u32[]{:S(2)}, u32[]{:S(2)}) async-start(bf16[16,48,256]{2,1,0:T(8,128)(2,1)} %conv.1), calls=%async_computation.1 | async-start | bytes 786432 | tf_op jit(solution)/shard_map/all_to_all | solution.py:428
  51.0 0.0 collective-permute-done
  51.0 2.0 %collective-permute-start.2 = (bf16[48,3072]{1,0:T(8,128)(2,1)}, bf16[48,3072]{1,0:T(8,128)(2,1)S(1)}, u32[]{:S(2)}, u32[]{:S(2)}) collective-permute-start(bf16[48,3072]{1,0:T(8,128)(2,1)} %collective-permute-done), channel_id=1, source_target_pairs={{0,4},{1,3},{2,6},{3,1},{4,0},{5,7},{6,2},{7,5},{8,12},{9,11},{10,... | collective-permute-start | bytes 884744 | tf_op jit(solution)/shard_map/ppermute | solution.py:300
  53.0 0.0 collective-permute-done.7
  53.0 0.1 collective-permute-start.9
  53.1 1.9 %collective-permute-start.8 = (bf16[48,3072]{1,0:T(8,128)(2,1)}, bf16[48,3072]{1,0:T(8,128)(2,1)S(1)}, u32[]{:S(2)}, u32[]{:S(2)}) collective-permute-start(bf16[48,3072]{1,0:T(8,128)(2,1)} %collective-permute-done.7), channel_id=1, source_target_pairs={{0,2},{1,5},{2,0},{3,7},{4,6},{5,1},{6,4},{7,3},{8,10},{9,13},{10,... | collective-permute-start | bytes 884744 | tf_op jit(solution)/shard_map/ppermute | solution.py:300
  55.0 0.0 collective-permute-done.1
  55.0 0.1 collective-permute-start.4
  55.1 0.0 collective-permute-done.11
  55.1 1.9 %collective-permute-start.12 = (bf16[48,3072]{1,0:T(8,128)(2,1)}, bf16[48,3072]{1,0:T(8,128)(2,1)S(1)}, u32[]{:S(2)}, u32[]{:S(2)}) collective-permute-start(bf16[48,3072]{1,0:T(8,128)(2,1)} %collective-permute-done.11), channel_id=1, source_target_pairs={{0,2},{1,5},{2,0},{3,7},{4,6},{5,1},{6,4},{7,3},{8,10},{9,13},{10,... | collective-permute-start | bytes 884744 | tf_op jit(solution)/shard_map/ppermute | solution.py:300
  57.1 7.5 %collective-permute-done.2 = bf16[48,3072]{1,0:T(8,128)(2,1)S(1)} collective-permute-done((bf16[48,3072]{1,0:T(8,128)(2,1)}, bf16[48,3072]{1,0:T(8,128)(2,1)S(1)}, u32[]{:S(2)}, u32[]{:S(2)}) %collective-permute-start.2) | collective-permute-done | bytes 294944 | tf_op jit(solution)/shard_map/ppermute | solution.py:300
  64.6 1.0 %collective-permute-start.5 = (bf16[48,3072]{1,0:T(8,128)(2,1)S(1)}, bf16[48,3072]{1,0:T(8,128)(2,1)S(1)}, u32[]{:S(2)}, u32[]{:S(2)}) collective-permute-start(bf16[48,3072]{1,0:T(8,128)(2,1)S(1)} %collective-permute-done.3), channel_id=1, source_target_pairs={{0,4},{1,3},{2,6},{3,1},{4,0},{5,7},{6,2},{7,5},{8,12},{9,11},{10,... | collective-permute-start | bytes 884744 | tf_op jit(solution)/shard_map/ppermute | solution.py:300
  65.6 5.3 %collective-permute-done.9 = bf16[48,3072]{1,0:T(8,128)(2,1)S(1)} collective-permute-done((bf16[48,3072]{1,0:T(8,128)(2,1)}, bf16[48,3072]{1,0:T(8,128)(2,1)S(1)}, u32[]{:S(2)}, u32[]{:S(2)}) %collective-permute-start.9) | collective-permute-done | bytes 294944 | tf_op jit(solution)/shard_map/ppermute | solution.py:300
  70.9 1.0 %collective-permute-start.13 = (bf16[48,3072]{1,0:T(8,128)(2,1)}, bf16[48,3072]{1,0:T(8,128)(2,1)}, u32[]{:S(2)}, u32[]{:S(2)}) collective-permute-start(bf16[48,3072]{1,0:T(8,128)(2,1)} %collective-permute-done.11), channel_id=1, source_target_pairs={{0,4},{1,3},{2,6},{3,1},{4,0},{5,7},{6,2},{7,5},{8,12},{9,11},{10,... | collective-permute-start | bytes 884744 | tf_op jit(solution)/shard_map/ppermute | solution.py:300
  71.9 0.0 collective-permute-done.8
  71.9 1.1 %collective-permute-start.10 = (bf16[48,3072]{1,0:T(8,128)(2,1)S(1)}, bf16[48,3072]{1,0:T(8,128)(2,1)}, u32[]{:S(2)}, u32[]{:S(2)}) collective-permute-start(bf16[48,3072]{1,0:T(8,128)(2,1)S(1)} %collective-permute-done.8), channel_id=1, source_target_pairs={{0,4},{1,3},{2,6},{3,1},{4,0},{5,7},{6,2},{7,5},{8,12},{9,11},{10,... | collective-permute-start | bytes 884744 | tf_op jit(solution)/shard_map/ppermute | solution.py:300
  73.0 0.0 collective-permute-done.4
  73.0 1.0 %collective-permute-start.6 = (bf16[48,3072]{1,0:T(8,128)(2,1)S(1)}, bf16[48,3072]{1,0:T(8,128)(2,1)}, u32[]{:S(2)}, u32[]{:S(2)}) collective-permute-start(bf16[48,3072]{1,0:T(8,128)(2,1)S(1)} %collective-permute-done.4), channel_id=1, source_target_pairs={{0,4},{1,3},{2,6},{3,1},{4,0},{5,7},{6,2},{7,5},{8,12},{9,11},{10,... | collective-permute-start | bytes 884744 | tf_op jit(solution)/shard_map/ppermute | solution.py:300
  73.9 4.4 %collective-permute-done.12 = bf16[48,3072]{1,0:T(8,128)(2,1)S(1)} collective-permute-done((bf16[48,3072]{1,0:T(8,128)(2,1)}, bf16[48,3072]{1,0:T(8,128)(2,1)S(1)}, u32[]{:S(2)}, u32[]{:S(2)}) %collective-permute-start.12) | collective-permute-done | bytes 294944 | tf_op jit(solution)/shard_map/ppermute | solution.py:300
  78.3 1.3 %collective-permute-start.14 = (bf16[48,3072]{1,0:T(8,128)(2,1)S(1)}, bf16[48,3072]{1,0:T(8,128)(2,1)}, u32[]{:S(2)}, u32[]{:S(2)}) collective-permute-start(bf16[48,3072]{1,0:T(8,128)(2,1)S(1)} %collective-permute-done.12), channel_id=1, source_target_pairs={{0,4},{1,3},{2,6},{3,1},{4,0},{5,7},{6,2},{7,5},{8,12},{9,11},{10,... | collective-permute-start | bytes 884744 | tf_op jit(solution)/shard_map/ppermute | solution.py:300
  79.6 0.0 collective-permute-done.5
  79.7 3.8 %collective-permute-done.10 = bf16[48,3072]{1,0:T(8,128)(2,1)} collective-permute-done((bf16[48,3072]{1,0:T(8,128)(2,1)S(1)}, bf16[48,3072]{1,0:T(8,128)(2,1)}, u32[]{:S(2)}, u32[]{:S(2)}) %collective-permute-start.10) | collective-permute-done | bytes 294944 | tf_op jit(solution)/shard_map/ppermute | solution.py:300
  83.5 0.0 collective-permute-done.13
  83.5 3.2 %collective-permute-done.6 = bf16[48,3072]{1,0:T(8,128)(2,1)} collective-permute-done((bf16[48,3072]{1,0:T(8,128)(2,1)S(1)}, bf16[48,3072]{1,0:T(8,128)(2,1)}, u32[]{:S(2)}, u32[]{:S(2)}) %collective-permute-start.6) | collective-permute-done | bytes 294944 | tf_op jit(solution)/shard_map/ppermute | solution.py:300
  86.6 3.2 %collective-permute-done.14 = bf16[48,3072]{1,0:T(8,128)(2,1)} collective-permute-done((bf16[48,3072]{1,0:T(8,128)(2,1)S(1)}, bf16[48,3072]{1,0:T(8,128)(2,1)}, u32[]{:S(2)}, u32[]{:S(2)}) %collective-permute-start.14) | collective-permute-done | bytes 294944 | tf_op jit(solution)/shard_map/ppermute | solution.py:300
  89.8 0.0 all-to-all-done.1.act_ref
  89.8 3.0 %mix.1 = (bf16[128,3072]{1,0:T(8,128)(2,1)S(1)}, f32[128,3072]{1,0:T(8,128)S(1)}) custom-call(s32[17]{0:T(128)S(1)} %compare_select_fusion.3.order_ref, bf16[16,48,256]{2,1,0:T(8,128)(2,1)S(1)} %all-to-all-done.1.act_ref, bf16[1,48,3072]{2,1,0:T(8,128)(2,1)S(1)} %bitcast.20, bf16[1,48,3072]{2,1,0:T(8,128)(2,1)} %bitcast.4.refs_1_, ...), custom_call_target="tpu_custom_call" | custom-call | flops 1207959552 | bytes 4718592 | tf_op jit(solution)/shard_map/mix/pallas_call | solution.py:354
  92.8 0.1 collective-permute-start.15
  92.8 2.3 %collective-permute-done.15.arrived_ref = bf16[128,3072]{1,0:T(8,128)(2,1)S(1)} collective-permute-done((bf16[128,3072]{1,0:T(8,128)(2,1)S(1)}, bf16[128,3072]{1,0:T(8,128)(2,1)S(1)}, u32[]{:S(2)}, u32[]{:S(2)}) %collective-permute-start.15) | collective-permute-done | bytes 786464 | tf_op jit(solution)/shard_map/ppermute | solution.py:430
  95.1 1.0 %finish.1 = bf16[128,1536]{1,0:T(8,128)(2,1)} custom-call(f32[128,3072]{1,0:T(8,128)S(1)} %get-tuple-element.13.ours_ref, bf16[128,3072]{1,0:T(8,128)(2,1)S(1)} %collective-permute-done.15.arrived_ref), custom_call_target="tpu_custom_call" | custom-call | flops 1572864 | bytes 2752512 | tf_op jit(solution)/shard_map/finish/pallas_call | solution.py:385
  (9 shorter events, 0.0 us)
Async XLA Ops:
  0.0 32.7 %copy-start = (f32[1536]{0:T(1024)S(1)}, f32[1536]{0:T(1024)}, u32[]{:S(2)}) copy-start(f32[1536]{0:T(1024)} %param.14) | copy-start | bytes 18436
  0.0 32.8 %copy-start.5 = (f32[11,3,384]{2,1,0:T(4,128)S(1)}, f32[11,3,384]{2,1,0:T(4,128)}, u32[]{:S(2)}) copy-start(f32[11,3,384]{2,1,0:T(4,128)} %constant.81.clone.tab_ref) | copy-start | bytes 152068
  0.0 32.8 %copy-start.4 = (f32[2,64]{1,0:T(2,128)S(1)}, f32[2,64]{1,0:T(2,128)}, u32[]{:S(2)}) copy-start(f32[2,64]{1,0:T(2,128)} %low_ref.1) | copy-start | bytes 1540
  0.0 32.8 %copy-start.3 = (f32[2,64]{1,0:T(2,128)S(1)}, f32[2,64]{1,0:T(2,128)}, u32[]{:S(2)}) copy-start(f32[2,64]{1,0:T(2,128)} %rates_ref.1) | copy-start | bytes 1540
  2.0 39.2 %copy-start.1 = (bf16[704,256]{1,0:T(8,128)(2,1)S(1)}, bf16[704,256]{1,0:T(8,128)(2,1)}, u32[]{:S(2)}) copy-start(bf16[704,256]{1,0:T(8,128)(2,1)} %constant.82.clone.refs_2_) | copy-start | bytes 1081348
  2.0 39.2 %all-to-all-start = ((bf16[32,48,128]{2,1,0:T(8,128)(2,1)}), bf16[32,48,128]{2,1,0:T(8,128)(2,1)S(1)}, u32[]{:S(2)}, u32[]{:S(2)}) async-start(bf16[32,48,128]{2,1,0:T(8,128)(2,1)} %bitcast.1), calls=%async_computation | async-start | bytes 786432 | tf_op jit(solution)/shard_map/all_to_all | solution.py:406
  9.3 17.9 %collective-permute-start.3 = (bf16[48,3072]{1,0:T(8,128)(2,1)}, bf16[48,3072]{1,0:T(8,128)(2,1)S(1)}, u32[]{:S(2)}, u32[]{:S(2)}) collective-permute-start(bf16[48,3072]{1,0:T(8,128)(2,1)} %param.15), channel_id=1, source_target_pairs={{0,8},{1,9},{2,10},{3,11},{4,12},{5,13},{6,14},{7,15},{8,16},{9,17... | collective-permute-start | bytes 884744 | tf_op jit(solution)/shard_map/ppermute | solution.py:300
  11.2 43.9 %collective-permute-start.1 = (bf16[48,3072]{1,0:T(8,128)(2,1)}, bf16[48,3072]{1,0:T(8,128)(2,1)S(1)}, u32[]{:S(2)}, u32[]{:S(2)}) collective-permute-start(bf16[48,3072]{1,0:T(8,128)(2,1)} %param.15), channel_id=1, source_target_pairs={{0,4},{1,3},{2,6},{3,1},{4,0},{5,7},{6,2},{7,5},{8,12},{9,11},{10,... | collective-permute-start | bytes 884744 | tf_op jit(solution)/shard_map/ppermute | solution.py:300
  12.6 38.4 %collective-permute-start = (bf16[48,3072]{1,0:T(8,128)(2,1)}, bf16[48,3072]{1,0:T(8,128)(2,1)}, u32[]{:S(2)}, u32[]{:S(2)}) collective-permute-start(bf16[48,3072]{1,0:T(8,128)(2,1)} %param.15), channel_id=1, source_target_pairs={{0,2},{1,5},{2,0},{3,7},{4,6},{5,1},{6,4},{7,3},{8,10},{9,13},{10,... | collective-permute-start | bytes 884744 | tf_op jit(solution)/shard_map/ppermute | solution.py:300
  14.1 38.9 %collective-permute-start.7 = (bf16[48,3072]{1,0:T(8,128)(2,1)}, bf16[48,3072]{1,0:T(8,128)(2,1)}, u32[]{:S(2)}, u32[]{:S(2)}) collective-permute-start(bf16[48,3072]{1,0:T(8,128)(2,1)} %param.15), channel_id=1, source_target_pairs={{0,24},{1,25},{2,26},{3,27},{4,28},{5,29},{6,30},{7,31},{8,0},{9,1... | collective-permute-start | bytes 884744 | tf_op jit(solution)/shard_map/ppermute | solution.py:300
  27.2 27.9 %collective-permute-start.11 = (bf16[48,3072]{1,0:T(8,128)(2,1)S(1)}, bf16[48,3072]{1,0:T(8,128)(2,1)}, u32[]{:S(2)}, u32[]{:S(2)}) collective-permute-start(bf16[48,3072]{1,0:T(8,128)(2,1)S(1)} %collective-permute-done.3), channel_id=1, source_target_pairs={{0,8},{1,9},{2,10},{3,11},{4,12},{5,13},{6,14},{7,15},{8,16},{9,17... | collective-permute-start | bytes 884744 | tf_op jit(solution)/shard_map/ppermute | solution.py:300
  41.1 48.7 %copy-start.2 = (bf16[48,3072]{1,0:T(8,128)(2,1)S(1)}, bf16[48,3072]{1,0:T(8,128)(2,1)}, u32[]{:S(2)}) copy-start(bf16[48,3072]{1,0:T(8,128)(2,1)} %param.15) | copy-start | bytes 884740
  45.3 44.5 %all-to-all-start.1 = ((bf16[16,48,256]{2,1,0:T(8,128)(2,1)}), bf16[16,48,256]{2,1,0:T(8,128)(2,1)S(1)}, u32[]{:S(2)}, u32[]{:S(2)}) async-start(bf16[16,48,256]{2,1,0:T(8,128)(2,1)} %conv.1), calls=%async_computation.1 | async-start | bytes 786432 | tf_op jit(solution)/shard_map/all_to_all | solution.py:428
  51.0 13.6 %collective-permute-start.2 = (bf16[48,3072]{1,0:T(8,128)(2,1)}, bf16[48,3072]{1,0:T(8,128)(2,1)S(1)}, u32[]{:S(2)}, u32[]{:S(2)}) collective-permute-start(bf16[48,3072]{1,0:T(8,128)(2,1)} %collective-permute-done), channel_id=1, source_target_pairs={{0,4},{1,3},{2,6},{3,1},{4,0},{5,7},{6,2},{7,5},{8,12},{9,11},{10,... | collective-permute-start | bytes 884744 | tf_op jit(solution)/shard_map/ppermute | solution.py:300
  53.0 17.9 %collective-permute-start.9 = (bf16[48,3072]{1,0:T(8,128)(2,1)}, bf16[48,3072]{1,0:T(8,128)(2,1)S(1)}, u32[]{:S(2)}, u32[]{:S(2)}) collective-permute-start(bf16[48,3072]{1,0:T(8,128)(2,1)} %collective-permute-done.7), channel_id=1, source_target_pairs={{0,4},{1,3},{2,6},{3,1},{4,0},{5,7},{6,2},{7,5},{8,12},{9,11},{10,... | collective-permute-start | bytes 884744 | tf_op jit(solution)/shard_map/ppermute | solution.py:300
  53.1 18.8 %collective-permute-start.8 = (bf16[48,3072]{1,0:T(8,128)(2,1)}, bf16[48,3072]{1,0:T(8,128)(2,1)S(1)}, u32[]{:S(2)}, u32[]{:S(2)}) collective-permute-start(bf16[48,3072]{1,0:T(8,128)(2,1)} %collective-permute-done.7), channel_id=1, source_target_pairs={{0,2},{1,5},{2,0},{3,7},{4,6},{5,1},{6,4},{7,3},{8,10},{9,13},{10,... | collective-permute-start | bytes 884744 | tf_op jit(solution)/shard_map/ppermute | solution.py:300
  55.0 17.9 %collective-permute-start.4 = (bf16[48,3072]{1,0:T(8,128)(2,1)S(1)}, bf16[48,3072]{1,0:T(8,128)(2,1)S(1)}, u32[]{:S(2)}, u32[]{:S(2)}) collective-permute-start(bf16[48,3072]{1,0:T(8,128)(2,1)S(1)} %collective-permute-done.3), channel_id=1, source_target_pairs={{0,2},{1,5},{2,0},{3,7},{4,6},{5,1},{6,4},{7,3},{8,10},{9,13},{10,... | collective-permute-start | bytes 884744 | tf_op jit(solution)/shard_map/ppermute | solution.py:300
  55.1 23.2 %collective-permute-start.12 = (bf16[48,3072]{1,0:T(8,128)(2,1)}, bf16[48,3072]{1,0:T(8,128)(2,1)S(1)}, u32[]{:S(2)}, u32[]{:S(2)}) collective-permute-start(bf16[48,3072]{1,0:T(8,128)(2,1)} %collective-permute-done.11), channel_id=1, source_target_pairs={{0,2},{1,5},{2,0},{3,7},{4,6},{5,1},{6,4},{7,3},{8,10},{9,13},{10,... | collective-permute-start | bytes 884744 | tf_op jit(solution)/shard_map/ppermute | solution.py:300
  64.6 15.0 %collective-permute-start.5 = (bf16[48,3072]{1,0:T(8,128)(2,1)S(1)}, bf16[48,3072]{1,0:T(8,128)(2,1)S(1)}, u32[]{:S(2)}, u32[]{:S(2)}) collective-permute-start(bf16[48,3072]{1,0:T(8,128)(2,1)S(1)} %collective-permute-done.3), channel_id=1, source_target_pairs={{0,4},{1,3},{2,6},{3,1},{4,0},{5,7},{6,2},{7,5},{8,12},{9,11},{10,... | collective-permute-start | bytes 884744 | tf_op jit(solution)/shard_map/ppermute | solution.py:300
  70.9 12.6 %collective-permute-start.13 = (bf16[48,3072]{1,0:T(8,128)(2,1)}, bf16[48,3072]{1,0:T(8,128)(2,1)}, u32[]{:S(2)}, u32[]{:S(2)}) collective-permute-start(bf16[48,3072]{1,0:T(8,128)(2,1)} %collective-permute-done.11), channel_id=1, source_target_pairs={{0,4},{1,3},{2,6},{3,1},{4,0},{5,7},{6,2},{7,5},{8,12},{9,11},{10,... | collective-permute-start | bytes 884744 | tf_op jit(solution)/shard_map/ppermute | solution.py:300
  71.9 11.6 %collective-permute-start.10 = (bf16[48,3072]{1,0:T(8,128)(2,1)S(1)}, bf16[48,3072]{1,0:T(8,128)(2,1)}, u32[]{:S(2)}, u32[]{:S(2)}) collective-permute-start(bf16[48,3072]{1,0:T(8,128)(2,1)S(1)} %collective-permute-done.8), channel_id=1, source_target_pairs={{0,4},{1,3},{2,6},{3,1},{4,0},{5,7},{6,2},{7,5},{8,12},{9,11},{10,... | collective-permute-start | bytes 884744 | tf_op jit(solution)/shard_map/ppermute | solution.py:300
  73.0 13.7 %collective-permute-start.6 = (bf16[48,3072]{1,0:T(8,128)(2,1)S(1)}, bf16[48,3072]{1,0:T(8,128)(2,1)}, u32[]{:S(2)}, u32[]{:S(2)}) collective-permute-start(bf16[48,3072]{1,0:T(8,128)(2,1)S(1)} %collective-permute-done.4), channel_id=1, source_target_pairs={{0,4},{1,3},{2,6},{3,1},{4,0},{5,7},{6,2},{7,5},{8,12},{9,11},{10,... | collective-permute-start | bytes 884744 | tf_op jit(solution)/shard_map/ppermute | solution.py:300
  78.3 11.5 %collective-permute-start.14 = (bf16[48,3072]{1,0:T(8,128)(2,1)S(1)}, bf16[48,3072]{1,0:T(8,128)(2,1)}, u32[]{:S(2)}, u32[]{:S(2)}) collective-permute-start(bf16[48,3072]{1,0:T(8,128)(2,1)S(1)} %collective-permute-done.12), channel_id=1, source_target_pairs={{0,4},{1,3},{2,6},{3,1},{4,0},{5,7},{6,2},{7,5},{8,12},{9,11},{10,... | collective-permute-start | bytes 884744 | tf_op jit(solution)/shard_map/ppermute | solution.py:300
  92.8 2.4 %collective-permute-start.15 = (bf16[128,3072]{1,0:T(8,128)(2,1)S(1)}, bf16[128,3072]{1,0:T(8,128)(2,1)S(1)}, u32[]{:S(2)}, u32[]{:S(2)}) collective-permute-start(bf16[128,3072]{1,0:T(8,128)(2,1)S(1)} %get-tuple-element.14), channel_id=1, source_target_pairs={{0,1},{1,0},{2,3},{3,2},{4,5},{5,4},{6,7},{7,6},{8,9},{9,8},{10,11... | collective-permute-start | bytes 2359304 | tf_op jit(solution)/shard_map/ppermute | solution.py:430
